TPU v7x, 256 devices: a whole 4x4x8 slice. The times are simulated.
256 devices in a mesh: group: 2 (over x_hi), seq: 16 (over x_lo, z), tensor: 8 (over y, core).
Axes of the slice: x: 4 (x_hi: 2, x_lo: 2; x = x_hi * 2 + x_lo), y: 4, z: 8, core: 2. Of those that a mesh axis runs over, the one named last changes fastest.
Arguments:
- tokens: bfloat16 [2, 2048, 8192], P('group', 'seq', 'tensor'), may hold values from -6 to 6
- frame_feats: bfloat16 [2, 512, 1280], P('group', 'seq'), may hold values from -6 to 6
- w_proj: bfloat16 [1280, 8192], P(None, 'tensor'), may hold values from -0.15625 to 0.15625
- frame_pos: int32 [2, 512], P('group', 'seq'), may hold values from 0 to 2047, as said below
- segments: int32 [2, 2048], P('group', 'seq'), may hold values from 0 to 3, never falling along the last dimension, each value on 1 to 1024 neighbouring positions
- signs: int32 [2, 2048], P('group', 'seq'), may hold values from 0 to 1
- w_x: bfloat16 [8192, 8192], P(('group', 'seq'), 'tensor'), may hold values from -0.0625 to 0.0625
- w_bc: bfloat16 [8192, 2048], P(('group', 'seq'), 'tensor'), may hold values from -0.0625 to 0.0625
- w_dt: bfloat16 [8192, 128], P(('group', 'seq'), 'tensor'), may hold values from -0.0625 to 0.0625
- dt_bias: float32 [128], P('tensor'), may hold values from -4 to -2
- decay_rate: float32 [128], P('tensor'), may hold values from 0.0001 to 1
- skip_gain: float32 [128], P('tensor'), may hold values from 0.5 to 6
- probe: bfloat16 [2, 2048, 8192], P('group', 'seq', 'tensor'), may hold values from -6 to 6
Outputs:
- adv_tokens: bfloat16 [2, 2048, 8192], P('group', 'seq', 'tensor')
- adv_frames: bfloat16 [2, 512, 8192], P('group', 'seq', 'tensor')
Inputs may be any that keep to these rules, and one draw needn't show every extreme that they name: `frame_pos`: within a sample the positions are distinct; frame token k * 32 + b * 2 + i (0 <= i < 2) lies in positions b * 128 to (b + 1) * 128 - 1. `segments`: document ids never fall along a sample.
All inputs are finite; a program needn't handle non-finite values.
Results may differ from a plain program's by a relative error of at most 0.0095.
Values may be sent and summed in bfloat16 or wider, within the bound.
No kernel may reach another device: no remote copies, remote signals or barrier semaphores. Data moves between devices by JAX's collectives and lax.ppermute only.
A program may use at most 128 MiB of HBM per device.

v0:
```python
import jax
import jax.numpy as jnp
from jax import lax
from jax.sharding import PartitionSpec as P

HEAD_DIM = 64
STATE = 128


precise = lax.Precision.HIGHEST


def from_behind(x, axis, by):
    size = lax.axis_size(axis)
    pairs = [(i, i + by) for i in range(size) if 0 <= i + by < size]
    return lax.ppermute(x, axis, pairs)


def carried_in_2(x, axis, combine, identity):
    size, mine = (lax.axis_size(axis), lax.axis_index(axis))
    everything = jax.tree.map(
        lambda part, kind: lax.all_gather(part.astype(kind), axis), x, (jnp.bfloat16, jnp.bfloat16)
    )
    start = jax.tree.map(
        lambda part, zero: jnp.broadcast_to(jnp.asarray(zero, part.dtype), part.shape), x, identity
    )

    def lap(k, before):
        reached = k < mine
        new = combine(
            before, jax.tree.map(lambda part, own: part[k].astype(own.dtype), everything, x)
        )
        return jax.tree.map(lambda a, b: jnp.where(reached, a, b), new, before)

    return lax.fori_loop(0, size, lap, start)


def carried_in_3(x, axis, combine, identity):
    size, mine = (lax.axis_size(axis), lax.axis_index(axis))
    everything = jax.tree.map(
        lambda part, kind: lax.all_gather(part.astype(kind), axis),
        x,
        jax.tree.map(lambda a: jnp.bfloat16 if a.dtype == jnp.float32 else a.dtype, x),
    )
    start = jax.tree.map(
        lambda part, zero: jnp.broadcast_to(jnp.asarray(zero, part.dtype), part.shape), x, identity
    )

    def lap(k, before):
        at = size - 1 - k
        reached = at > mine
        new = combine(
            before, jax.tree.map(lambda part, own: part[at].astype(own.dtype), everything, x)
        )
        return jax.tree.map(lambda a, b: jnp.where(reached, a, b), new, before)

    return lax.fori_loop(0, size, lap, start)


def split_proj(proj_x, proj_bc, proj_dt, dt_bias):
    count = proj_x.shape[0]
    values = proj_x.reshape(count, -1, HEAD_DIM)
    pairs = proj_bc.reshape(count, -1, 2, STATE)
    step_sizes = jax.nn.softplus(proj_dt + dt_bias[None, :])
    return (values, pairs[:, :, 0], pairs[:, :, 1], step_sizes)


def block_state(proj_x, proj_bc, proj_dt, dt_bias, decay_rate, segment, seg_prev):
    values, b_proj, c_proj, step_sizes = split_proj(proj_x, proj_bc, proj_dt, dt_bias)
    repeat = values.shape[1] // b_proj.shape[1]
    log_decay = jnp.cumsum(-step_sizes * decay_rate[None, :], axis=0)
    end_decay = log_decay[-1]
    same_end = (segment == segment[-1])[:, None]
    tail_weight = jnp.where(same_end, jnp.exp(end_decay[None, :] - log_decay), 0.0) * step_sizes
    b_heads = jnp.repeat(b_proj, repeat, axis=1)
    end_states = jnp.einsum("sh,shp,shn->hpn", tail_weight, values, b_heads, precision=precise)
    carry_decay = jnp.where(segment[-1] == seg_prev, jnp.exp(end_decay), 0.0)
    return (end_states, carry_decay)


def block_loss(
    proj_x, proj_bc, proj_dt, dt_bias, decay_rate, skip_gain, segment, seg_prev, carried_in, probe
):
    values, b_proj, c_proj, step_sizes = split_proj(proj_x, proj_bc, proj_dt, dt_bias)
    repeat = values.shape[1] // b_proj.shape[1]
    count = values.shape[0]
    log_decay = jnp.cumsum(-step_sizes * decay_rate[None, :], axis=0)
    position = jnp.arange(count)
    visible = (segment[:, None] == segment[None, :]) & (position[:, None] >= position[None, :])
    visible = visible[:, :, None]
    gap_decay = log_decay[:, None, :] - log_decay[None, :, :]
    decay = jnp.where(visible, jnp.exp(jnp.where(visible, gap_decay, 0.0)), 0.0)
    scores = jnp.einsum("tgn,sgn->tsg", c_proj, b_proj, precision=precise)
    scores = jnp.repeat(scores, repeat, axis=2)
    mixed = decay * scores * step_sizes[None, :, :]
    within = jnp.einsum("tsh,shp->thp", mixed, values, precision=precise)
    c_heads = jnp.repeat(c_proj, repeat, axis=1)
    carry_scale = jnp.where((segment == seg_prev)[:, None], jnp.exp(log_decay), 0.0)
    carried = (
        jnp.einsum("thn,hpn->thp", c_heads, carried_in, precision=precise) * carry_scale[:, :, None]
    )
    result = within + carried + skip_gain[None, :, None] * values
    return jnp.sum(result.reshape(count, -1) * probe.astype(jnp.float32))


def combine(earlier, later):
    return (earlier[0] * later[0], later[1] + later[0][:, None, None] * earlier[1])


def body(
    tokens,
    frame_feats,
    w_proj,
    frame_pos,
    segments,
    signs,
    w_x,
    w_bc,
    w_dt,
    dt_bias,
    decay_rate,
    skip_gain,
    probe,
):
    rows = tokens.shape[1]
    seq_count = lax.axis_size("seq")
    own_index = lax.axis_index("seq")
    frame_emb = jnp.dot(frame_feats[0], w_proj, preferred_element_type=jnp.float32).astype(
        jnp.bfloat16
    )
    arrived, arrived_pos = (
        lax.all_to_all(frame_emb, "seq", split_axis=0, concat_axis=0, tiled=True),
        lax.all_to_all(frame_pos[0], "seq", split_axis=0, concat_axis=0, tiled=True),
    )
    local_pos = arrived_pos - own_index * rows
    merged = tokens[0].at[local_pos].set(arrived)
    segment = segments[0]
    edge_ids = from_behind(segment[-1:], "seq", 1)
    seg_prev = edge_ids[0]
    features = lax.all_gather(merged, "tensor", axis=1, tiled=True)
    whole_x, whole_bc, whole_dt = (
        lax.all_gather(w_x, ("group", "seq"), axis=0, tiled=True),
        lax.all_gather(w_bc, ("group", "seq"), axis=0, tiled=True),
        lax.all_gather(w_dt, ("group", "seq"), axis=0, tiled=True),
    )
    proj_x = jnp.dot(features, whole_x, preferred_element_type=jnp.float32)
    proj_bc = jnp.dot(features, whole_bc, preferred_element_type=jnp.float32)
    proj_dt = jnp.dot(features, whole_dt, preferred_element_type=jnp.float32)

    def state_of(part_x, part_bc, part_dt):
        return block_state(part_x, part_bc, part_dt, dt_bias, decay_rate, segment, seg_prev)

    (end_states, carry_decay), pull_state = jax.vjp(state_of, proj_x, proj_bc, proj_dt)
    identity = (jnp.ones_like(carry_decay), jnp.zeros_like(end_states))
    _, entering = carried_in_2((carry_decay, end_states), "seq", combine, identity)

    def loss_of(part_x, part_bc, part_dt, carried_in):
        return block_loss(
            part_x,
            part_bc,
            part_dt,
            dt_bias,
            decay_rate,
            skip_gain,
            segment,
            seg_prev,
            carried_in,
            probe[0],
        )

    _, pull_loss = jax.vjp(loss_of, proj_x, proj_bc, proj_dt, entering)
    loss_gx, loss_gbc, loss_gdt, local_grad = pull_loss(jnp.ones((), jnp.float32))
    _, leaving_grad = carried_in_3((carry_decay, local_grad), "seq", combine, identity)
    decay_grad = jnp.sum(leaving_grad * entering, axis=(1, 2))
    state_gx, state_gbc, state_gdt = pull_state((leaving_grad, decay_grad))
    grad_x = (loss_gx + state_gx).astype(jnp.bfloat16)
    grad_bc = (loss_gbc + state_gbc).astype(jnp.bfloat16)
    grad_dt = (loss_gdt + state_gdt).astype(jnp.bfloat16)
    partial_value = jnp.dot(grad_x, whole_x.T, preferred_element_type=jnp.float32)
    partial_value = partial_value + jnp.dot(grad_bc, whole_bc.T, preferred_element_type=jnp.float32)
    partial_value = partial_value + jnp.dot(grad_dt, whole_dt.T, preferred_element_type=jnp.float32)
    gradient = lax.psum_scatter(
        partial_value.astype(jnp.bfloat16), "tensor", scatter_dimension=1, tiled=True
    ).astype(jnp.float32)
    entries = rows * seq_count * gradient.shape[1] * lax.axis_size("tensor")
    squares = lax.psum(jnp.sum(gradient * gradient), ("seq", "tensor"))
    grad_scale = jnp.sqrt(squares / entries + 1e-06)
    direction = (2 * signs[0] - 1).astype(jnp.float32)[:, None]
    adv = (merged.astype(jnp.float32) + 0.5 * direction * gradient / grad_scale).astype(
        jnp.bfloat16
    )
    picked = adv[local_pos]
    returned = lax.all_to_all(picked, "seq", split_axis=0, concat_axis=0, tiled=True)
    return (adv[None], returned[None])


def solution(mesh):
    return jax.shard_map(
        body,
        mesh=mesh,
        in_specs=(
            P("group", "seq", "tensor"),
            P("group", "seq", None),
            P(None, "tensor"),
            P("group", "seq"),
            P("group", "seq"),
            P("group", "seq"),
            P(("group", "seq"), "tensor"),
            P(("group", "seq"), "tensor"),
            P(("group", "seq"), "tensor"),
            P("tensor"),
            P("tensor"),
            P("tensor"),
            P("group", "seq", "tensor"),
        ),
        out_specs=(P("group", "seq", "tensor"), P("group", "seq", "tensor")),
        check_vma=False,
    )
```

profile of v0, /device:TPU:4, one launch (start us, length us, event | category | flops | bytes accessed | tf_op | source)
XLA Modules:
  0.0 862.1 jit_solution(18328553212502681341)
XLA Ops:
  10.9 9.2 %all-to-all-start = ((s32[16,2,1]{1,2,0:T(1,128)}), s32[16,2,1]{1,2,0:T(1,128)S(1)}, u32[]{:S(2)}, u32[]{:S(2)}) async-start(s32[16,2,1]{1,2,0:T(1,128)} %bitcast.1), calls=%async_computation | async-start | bytes 16384 | tf_op jit(solution)/shard_map/all_to_all | solution.py:133
  22.2 6.3 all-to-all-done
  28.5 3.5 all-to-all-start.1
  32.2 8.3 all-to-all-done.1
  43.6 3.4 collective-permute-start
  47.2 40.8 %all_gather.31 = bf16[8192,16]{0,1:T(8,128)(2,1)S(1)} all-gather(bf16[256,16]{0,1:T(8,128)(2,1)S(1)} %copy-done.20), channel_id=1, replica_groups=mesh['group'=2,'seq'=16,'tensor'=8] {'group','seq'}, dimensions={0}, use_global_device_ids=true | all-gather | bytes 270336 | tf_op jit(solution)/shard_map/all_gather | solution.py:144
  88.1 1.9 broadcast_compare_fusion
  89.9 2.3 negate_multiply_fusion
  92.6 57.7 %all-gather.11.cloned.1.call-done = bf16[8192,256]{1,0:T(8,128)(2,1)} async-done(((bf16[256,256]{1,0:T(8,128)(2,1)}), bf16[8192,256]{1,0:T(8,128)(2,1)}) %all-gather.11.cloned.1.call-update) | async-done | bytes 4194320 | tf_op jit(solution)/shard_map/all_gather | solution.py:143
  150.3 3.5 fusion.60
  154.0 1.7 convolution_convert_fusion.1
  157.8 31.9 %all-gather.2 = bf16[16,1,16]{2,1,0:T(2,128)(2,1)S(1)} all-gather(bf16[1,1,16]{2,1,0:T(2,128)(2,1)S(1)} %bitcast.150), channel_id=1, replica_groups=mesh['group'=2,'seq'=16,'tensor'=8] {'seq'}, dimensions={0}, use_global_device_ids=true | all-gather | bytes 544 | tf_op jit(solution)/shard_map/all_gather | solution.py:41
  191.1 38.9 %all-gather.15.cloned.1.call-done = bf16[256,64,128]{2,1,0:T(8,128)(2,1)} async-done(((bf16[16,64,128]{2,1,0:T(8,128)(2,1)}), bf16[256,64,128]{2,1,0:T(8,128)(2,1)}) %all-gather.15.cloned.1.call-update) | async-done | bytes 4194320 | tf_op jit(solution)/shard_map/all_gather | solution.py:41
  230.0 37.9 %while.30 = (s32[]{:T(128)}, f32[16,64,128]{2,1,0:T(8,128)S(1)}, s32[]{:T(128)}, bf16[16,16,64,128]{3,2,1,0:T(8,128)(2,1)}, bf16[16,16]{1,0:T(8,128)(2,1)}, /*index=5*/s32[]{:T(128)}, s32[]{:T(128)}, s32[]{:T(128)}, s32[]{:T(128)}) while((s32[]{:T(128)}, f32[16,64,128]{2,1,0:T(8,128)S(1)}, s32[]{:T(128)}, ...), condition=%wide.region_3.5_spmd.clone, body=%wide.region_2.4_spmd.clone.sunk | while | flops 655384 | bytes 1311055 | solution.py:57
  267.9 100.2 %all-gather.13.cloned.1.call-done = bf16[8192,1024]{1,0:T(8,128)(2,1)} async-done(((bf16[256,1024]{1,0:T(8,128)(2,1)}), bf16[8192,1024]{1,0:T(8,128)(2,1)}) %all-gather.13.cloned.1.call-update) | async-done | bytes 16777232 | tf_op jit(solution)/shard_map/all_gather | solution.py:142
  368.1 13.8 %fusion.62 = f32[128,1024]{0,1:T(8,128)} fusion(bf16[128,8192]{1,0:T(8,128)(2,1)} %all-gather.9.cloned.1.call-done, bf16[8192,1024]{1,0:T(8,128)(2,1)} %all-gather.13.cloned.1.call-done), kind=kOutput, calls=%fused_computation.113 | convolution fusion | flops 2147483648 | bytes 19398656 | tf_op jit(solution)/shard_map/dot_general | solution.py:146
  381.9 3.9 multiply_reduce_fusion.2
  386.4 2.0 fusion.58
  389.0 2.7 convolution_convert_fusion
  397.2 3.2 fusion.14
  401.4 1.6 convolution_bitcast_fusion.4
  404.7 13.6 %fusion.61 = f32[128,8192]{1,0:T(8,128)} fusion(bf16[128,1024]{0,1:T(8,128)(2,1)} %bitcast.143, bf16[8192,1024]{1,0:T(8,128)(2,1)} %all-gather.13.cloned.1.call-done), kind=kOutput, calls=%fused_computation.112 | convolution fusion | flops 2147483648 | bytes 21233664 | tf_op jit(solution)/shard_map/dot_general | solution.py:179
  418.3 48.1 %all-gather.17.cloned.1.call-done = bf16[256,64,128]{2,1,0:T(8,128)(2,1)} async-done(((bf16[16,64,128]{2,1,0:T(8,128)(2,1)}), bf16[256,64,128]{2,1,0:T(8,128)(2,1)}) %all-gather.17.cloned.1.call-update) | async-done | bytes 4194320 | tf_op jit(solution)/shard_map/all_gather | solution.py:22
  466.4 38.2 %while.31 = (s32[]{:T(128)}, f32[16,64,128]{2,1,0:T(8,128)S(1)}, s32[]{:T(128)}, bf16[16,16,64,128]{3,2,1,0:T(8,128)(2,1)}, bf16[16,16]{1,0:T(8,128)(2,1)}, /*index=5*/s32[]{:T(128)}, s32[]{:T(128)}) while((s32[]{:T(128)}, f32[16,64,128]{2,1,0:T(8,128)S(1)}, s32[]{:T(128)}, bf16[16,16,64,128]{3,2,1,0:T(8,128)(2,1)}, ...), condition=%wide.region_5.7_spmd.clone, body=%wide.region_4.6_spmd.clone.sunk | while | flops 655380 | bytes 1310993 | solution.py:35
  504.5 1.7 convolution_bitcast_fusion.6
  507.5 2.7 fusion.7
  517.3 5.1 convolution_add_fusion.1
  522.4 2.2 fusion.2
  524.6 34.6 %reduce-scatter.2.cloned.1.call-done = bf16[128,1024]{1,0:T(8,128)(2,1)} async-done(((bf16[128,8192]{1,0:T(8,128)(2,1)}), bf16[128,1024]{1,0:T(8,128)(2,1)}) %reduce-scatter.2.cloned.1.call-update) | async-done | bytes 262160 | tf_op jit(solution)/shard_map/reduce_scatter | solution.py:182
  559.3 1.7 fusion.18
  561.0 280.0 %psum.7 = f32[]{:T(128)} all-reduce(f32[]{:T(128)} %fusion.18), channel_id=1, replica_groups=mesh['group'=2,'seq'=16,'tensor'=8] {'seq','tensor'}, use_global_device_ids=true, to_apply=%region_17.19 | all-reduce | flops 1 | bytes 8 | tf_op jit(solution)/shard_map/psum | solution.py:186
  843.5 11.1 %all_to_all.30 = bf16[16,2,1024]{2,1,0:T(2,128)(2,1)S(1)} all-to-all(bf16[16,2,1024]{2,1,0:T(2,128)(2,1)S(1)} %all_to_all.25), channel_id=1, replica_groups=mesh['group'=2,'seq'=16,'tensor'=8] {'seq'}, dimensions={0} | all-to-all | bytes 131072 | tf_op jit(solution)/shard_map/all_to_all | solution.py:193
  (194 shorter events, 107.2 us)
Async XLA Ops:
  7.2 12.9 %copy-start = (bf16[1280,1024]{1,0:T(8,128)(2,1)S(1)}, bf16[1280,1024]{1,0:T(8,128)(2,1)}, u32[]{:S(2)}) copy-start(bf16[1280,1024]{1,0:T(8,128)(2,1)} %param.20) | copy-start | bytes 7864324
  7.2 35.8 %copy-start.24 = (s32[1,128]{1,0:T(1,128)S(1)}, s32[1,128]{1,0:T(1,128)}, u32[]{:S(2)}) copy-start(s32[1,128]{1,0:T(1,128)} %param.22) | copy-start | bytes 1540
  7.2 40.0 %copy-start.20 = (bf16[256,16]{0,1:T(8,128)(2,1)S(1)}, bf16[256,16]{0,1:T(8,128)(2,1)}, u32[]{:S(2)}) copy-start(bf16[256,16]{0,1:T(8,128)(2,1)} %param.26) | copy-start | bytes 24580
  7.2 82.7 %copy-start.30 = (f32[16]{0:T(128)S(1)}, f32[16]{0:T(128)}, u32[]{:S(2)}) copy-start(f32[16]{0:T(128)} %param.27) | copy-start | bytes 196
  7.2 82.7 %copy-start.26 = (f32[16]{0:T(128)S(1)}, f32[16]{0:T(128)}, u32[]{:S(2)}) copy-start(f32[16]{0:T(128)} %param.28) | copy-start | bytes 196
  7.2 39.8 %copy-start.10 = (bf16[1,128,1024]{2,1,0:T(8,128)(2,1)S(1)}, bf16[1,128,1024]{2,1,0:T(8,128)(2,1)}, u32[]{:S(2)}) copy-start(bf16[1,128,1024]{2,1,0:T(8,128)(2,1)} %param.30) | copy-start | bytes 786436
  10.9 17.6 %all-to-all-start = ((s32[16,2,1]{1,2,0:T(1,128)}), s32[16,2,1]{1,2,0:T(1,128)S(1)}, u32[]{:S(2)}, u32[]{:S(2)}) async-start(s32[16,2,1]{1,2,0:T(1,128)} %bitcast.1), calls=%async_computation | async-start | bytes 16384 | tf_op jit(solution)/shard_map/all_to_all | solution.py:133
  28.5 12.0 %all-to-all-start.1 = ((bf16[16,2,1024]{2,1,0:T(2,128)(2,1)}), bf16[16,2,1024]{2,1,0:T(2,128)(2,1)S(1)}, u32[]{:S(2)}, u32[]{:S(2)}) async-start(bf16[16,2,1024]{2,1,0:T(2,128)(2,1)} %all_to_all.22), calls=%async_computation.1 | async-start | bytes 131072 | tf_op jit(solution)/shard_map/all_to_all | solution.py:132
  32.0 57.9 %all-gather.9.cloned.1.call-start = ((), (), s32[]{:S(2)}) async-start(), calls=%async_computation.4 | async-start | bytes 2359296 | tf_op jit(solution)/shard_map/all_gather | solution.py:140
  32.2 60.4 %copy-start.28 = (s32[32]{0:T(128)}, s32[32]{0:T(128)S(1)}, u32[]{:S(2)}) copy-start(s32[32]{0:T(128)S(1)} %fusion.54) | copy-start | bytes 388
  42.2 108.1 %all-gather.11.cloned.1.call-start = ((), (), s32[]{:S(2)}) async-start(), calls=%async_computation.5 | async-start | bytes 4325376 | tf_op jit(solution)/shard_map/all_gather | solution.py:143
  42.9 187.1 %all-gather.15.cloned.1.call-start = ((), (), s32[]{:S(2)}) async-start(), calls=%async_computation.8 | async-start | bytes 4456448 | tf_op jit(solution)/shard_map/all_gather | solution.py:41
  43.6 44.4 %collective-permute-start = (s32[1]{0:T(128)}, s32[1]{0:T(128)}, u32[]{:S(2)}, u32[]{:S(2)}) collective-permute-start(s32[1]{0:T(128)} %bitcast.14), channel_id=1, source_target_pairs={{0,8},{8,16},{16,24},{24,32},{32,40},{40,48},{48,56},{56,64},{64,7... | collective-permute-start | bytes 20 | tf_op jit(solution)/shard_map/ppermute | solution.py:16
  88.1 65.7 %copy-start.6 = (bf16[8192,16]{0,1:T(8,128)(2,1)}, bf16[8192,16]{0,1:T(8,128)(2,1)S(1)}, u32[]{:S(2)}) copy-start(bf16[8192,16]{0,1:T(8,128)(2,1)S(1)} %all_gather.31) | copy-start | bytes 786436
  89.9 63.9 %copy-start.25 = (pred[128]{0:T(512)(128)(4,1)}, pred[128]{0:T(512)(128)(4,1)S(1)}, u32[]{:S(2)}) copy-start(pred[128]{0:T(512)(128)(4,1)S(1)} %get-tuple-element.301) | copy-start | bytes 388
  92.6 63.8 %copy-start.16 = (f32[128,16]{0,1:T(8,128)}, f32[128,16]{0,1:T(8,128)S(1)}, u32[]{:S(2)}) copy-start(f32[128,16]{0,1:T(8,128)S(1)} %exponential_select_fusion) | copy-start | bytes 24580
  155.7 212.4 %all-gather.13.cloned.1.call-start = ((), (), s32[]{:S(2)}) async-start(), calls=%async_computation.6 | async-start | bytes 17301504 | tf_op jit(solution)/shard_map/all_gather | solution.py:142
  156.3 310.1 %all-gather.17.cloned.1.call-start = ((), (), s32[]{:S(2)}) async-start(), calls=%async_computation.9 | async-start | bytes 4456448 | tf_op jit(solution)/shard_map/all_gather | solution.py:22
  267.9 114.1 %copy-start.1 = (f32[16,64,128]{2,1,0:T(8,128)}, f32[16,64,128]{2,1,0:T(8,128)S(1)}, u32[]{:S(2)}) copy-start(f32[16,64,128]{2,1,0:T(8,128)S(1)} %get-tuple-element.231) | copy-start | bytes 1572868
  391.7 167.5 %reduce-scatter.2.cloned.1.call-start = ((), (), s32[]{:S(2)}) async-start(), calls=%async_computation.7 | async-start | bytes 2359296 | tf_op jit(solution)/shard_map/reduce_scatter | solution.py:182
  397.2 5.8 copy-start.9
  397.2 5.8 copy-start.17
  397.2 5.8 copy-start.18
  397.2 5.8 copy-start.21
  397.2 5.8 copy-start.31
  517.2 5.1 copy-start.7
  517.2 5.1 copy-start.13
  517.2 5.1 copy-start.19
  517.2 5.1 copy-start.22
  522.4 38.6 %copy-start.29 = (s32[32]{0:T(128)S(1)}, s32[32]{0:T(128)}, u32[]{:S(2)}) copy-start(s32[32]{0:T(128)} %copy-done.28) | copy-start | bytes 388
  522.4 319.3 %copy-start.5 = (bf16[128,1024]{1,0:T(8,128)(2,1)S(1)}, bf16[128,1024]{1,0:T(8,128)(2,1)}, u32[]{:S(2)}) copy-start(bf16[128,1024]{1,0:T(8,128)(2,1)} %copy-done.4) | copy-start | bytes 786436
  842.8 12.4 %copy-start.8 = (bf16[128,1024]{1,0:T(8,128)(2,1)}, bf16[128,1024]{1,0:T(8,128)(2,1)S(1)}, u32[]{:S(2)}) copy-start(bf16[128,1024]{1,0:T(8,128)(2,1)S(1)} %fusion.17) | copy-start | bytes 786436
  (10 other events, 31.2 us)
Sparse Core Ops, SparseCore 0:
  42.3 24.8 all-gather.8
  69.7 80.4 all-gather.10
  155.8 74.0 all-gather.14
  232.4 135.6 all-gather.12
  391.9 74.4 all-gather.16
  524.7 34.5 reduce-scatter.1
where the time goes:
time: 865 us; the launch traced here: 862 us
  blocking collectives  364 us (42%)
  waiting for transfers between devices  295 us (34%)
  other arithmetic  91.9 us (11%)
  matrix products  64 us (7%)
  starting transfers between devices  16.6 us (2%)
  between operations  16.6 us (2%)
  local copies, waits for them, and re-layouts  13.1 us (2%)
    psum x1, blocking collectives, body(): squares = lax.psum(jnp.sum(gradient * gradient), ('seq', 'tensor'))  280 us
    all_gather x1, waiting for transfers between devices, body(): lax.all_gather(w_x, ('group', 'seq'), axis=0, tiled=True)  100 us
    all_gather x1, waiting for transfers between devices, body(): lax.all_gather(w_bc, ('group', 'seq'), axis=0, tiled=True)  57.7 us
    all_gather x1, waiting for transfers between devices, carried_in_2(): lax.all_gather(part.astype(kind), axis)  48.1 us
    all_gather x1, blocking collectives, body(): lax.all_gather(w_dt, ('group', 'seq'), axis=0, tiled=True)  40.8 us
    all_gather x1, waiting for transfers between devices, carried_in_3(): lax.all_gather(part.astype(kind), axis)  38.9 us
    select_n x32, other arithmetic, lap(): return jax.tree.map(lambda a, b: jnp.where(reached, a, b), new, before)  35 us
    reduce_scatter x1, waiting for transfers between devices, body(): lax.psum_scatter(partial_value.astype(jnp.bfloat16), 'tensor', scatter_di...  34.6 us
  transfers between devices with their start and end apart: 9, of which 7 were waited for; matrix products, arithmetic and copies ran while one was open for 8% of the time, Pallas kernels for 0%

commit v1 on v0

v1 whole, which is shorter than its diff:
```python
import jax
import jax.numpy as jnp
from jax import lax
from jax.sharding import Mesh, PartitionSpec as P

HEAD_DIM = 64
SEQ = ("x_lo", "z")
TENSOR = ("y", "core")
STATE = 128


precise = lax.Precision.HIGHEST


def from_behind(x, axis, by):
    size = lax.axis_size(axis)
    pairs = [(i, i + by) for i in range(size) if 0 <= i + by < size]
    return lax.ppermute(x, axis, pairs)


def carried_in(x, axis, later):
    size, mine = (lax.axis_size(axis), lax.axis_index(axis))
    decays, states = jax.tree.map(lambda part: lax.all_gather(part.astype(jnp.bfloat16), axis), x)
    decays = decays.astype(jnp.float32)
    weights = [None] * size
    run = jnp.ones_like(decays[0])
    for k in range(size) if later else reversed(range(size)):
        reached = (k > mine) if later else (k < mine)
        weights[k] = jnp.where(reached, run, 0.0)
        run = jnp.where(reached, run * decays[k], run)
    weights = jnp.stack(weights)
    return jnp.sum(weights[:, :, None, None] * states.astype(jnp.float32), axis=0)


def split_proj(proj_x, proj_bc, proj_dt, dt_bias):
    count = proj_x.shape[0]
    values = proj_x.reshape(count, -1, HEAD_DIM)
    pairs = proj_bc.reshape(count, -1, 2, STATE)
    step_sizes = jax.nn.softplus(proj_dt + dt_bias[None, :])
    return (values, pairs[:, :, 0], pairs[:, :, 1], step_sizes)


def block_state(proj_x, proj_bc, proj_dt, dt_bias, decay_rate, segment, seg_prev):
    values, b_proj, c_proj, step_sizes = split_proj(proj_x, proj_bc, proj_dt, dt_bias)
    repeat = values.shape[1] // b_proj.shape[1]
    log_decay = jnp.cumsum(-step_sizes * decay_rate[None, :], axis=0)
    end_decay = log_decay[-1]
    same_end = (segment == segment[-1])[:, None]
    tail_weight = jnp.where(same_end, jnp.exp(end_decay[None, :] - log_decay), 0.0) * step_sizes
    b_heads = jnp.repeat(b_proj, repeat, axis=1)
    end_states = jnp.einsum("sh,shp,shn->hpn", tail_weight, values, b_heads, precision=precise)
    carry_decay = jnp.where(segment[-1] == seg_prev, jnp.exp(end_decay), 0.0)
    return (end_states, carry_decay)


def block_loss(
    proj_x, proj_bc, proj_dt, dt_bias, decay_rate, skip_gain, segment, seg_prev, carried_in, probe
):
    values, b_proj, c_proj, step_sizes = split_proj(proj_x, proj_bc, proj_dt, dt_bias)
    repeat = values.shape[1] // b_proj.shape[1]
    count = values.shape[0]
    log_decay = jnp.cumsum(-step_sizes * decay_rate[None, :], axis=0)
    position = jnp.arange(count)
    visible = (segment[:, None] == segment[None, :]) & (position[:, None] >= position[None, :])
    visible = visible[:, :, None]
    gap_decay = log_decay[:, None, :] - log_decay[None, :, :]
    decay = jnp.where(visible, jnp.exp(jnp.where(visible, gap_decay, 0.0)), 0.0)
    scores = jnp.einsum("tgn,sgn->tsg", c_proj, b_proj, precision=precise)
    scores = jnp.repeat(scores, repeat, axis=2)
    mixed = decay * scores * step_sizes[None, :, :]
    within = jnp.einsum("tsh,shp->thp", mixed, values, precision=precise)
    c_heads = jnp.repeat(c_proj, repeat, axis=1)
    carry_scale = jnp.where((segment == seg_prev)[:, None], jnp.exp(log_decay), 0.0)
    carried = (
        jnp.einsum("thn,hpn->thp", c_heads, carried_in, precision=precise) * carry_scale[:, :, None]
    )
    result = within + carried + skip_gain[None, :, None] * values
    return jnp.sum(result.reshape(count, -1) * probe.astype(jnp.float32))


def body(
    tokens,
    frame_feats,
    w_proj,
    frame_pos,
    segments,
    signs,
    w_x,
    w_bc,
    w_dt,
    dt_bias,
    decay_rate,
    skip_gain,
    probe,
):
    rows = tokens.shape[1]
    seq_count = lax.axis_size(SEQ)
    own_index = lax.axis_index(SEQ)
    frame_emb = jnp.dot(frame_feats[0], w_proj, preferred_element_type=jnp.float32).astype(
        jnp.bfloat16
    )
    arrived, arrived_pos = (
        lax.all_to_all(frame_emb, SEQ, split_axis=0, concat_axis=0, tiled=True),
        lax.all_to_all(frame_pos[0], SEQ, split_axis=0, concat_axis=0, tiled=True),
    )
    local_pos = arrived_pos - own_index * rows
    merged = tokens[0].at[local_pos].set(arrived)
    segment = segments[0]
    edge_ids = from_behind(segment[-1:], SEQ, 1)
    seg_prev = edge_ids[0]
    features = lax.all_gather(merged, TENSOR, axis=1, tiled=True)
    whole_x, whole_bc, whole_dt = (
        lax.all_gather(w_x, ("x_hi",) + SEQ, axis=0, tiled=True),
        lax.all_gather(w_bc, ("x_hi",) + SEQ, axis=0, tiled=True),
        lax.all_gather(w_dt, ("x_hi",) + SEQ, axis=0, tiled=True),
    )
    proj_x = jnp.dot(features, whole_x, preferred_element_type=jnp.float32)
    proj_bc = jnp.dot(features, whole_bc, preferred_element_type=jnp.float32)
    proj_dt = jnp.dot(features, whole_dt, preferred_element_type=jnp.float32)

    def state_of(part_x, part_bc, part_dt):
        return block_state(part_x, part_bc, part_dt, dt_bias, decay_rate, segment, seg_prev)

    (end_states, carry_decay), pull_state = jax.vjp(state_of, proj_x, proj_bc, proj_dt)
    entering = carried_in((carry_decay, end_states), SEQ, False)

    def loss_of(part_x, part_bc, part_dt, carried_in):
        return block_loss(
            part_x,
            part_bc,
            part_dt,
            dt_bias,
            decay_rate,
            skip_gain,
            segment,
            seg_prev,
            carried_in,
            probe[0],
        )

    _, pull_loss = jax.vjp(loss_of, proj_x, proj_bc, proj_dt, entering)
    loss_gx, loss_gbc, loss_gdt, local_grad = pull_loss(jnp.ones((), jnp.float32))
    leaving_grad = carried_in((carry_decay, local_grad), SEQ, True)
    decay_grad = jnp.sum(leaving_grad * entering, axis=(1, 2))
    state_gx, state_gbc, state_gdt = pull_state((leaving_grad, decay_grad))
    grad_x = (loss_gx + state_gx).astype(jnp.bfloat16)
    grad_bc = (loss_gbc + state_gbc).astype(jnp.bfloat16)
    grad_dt = (loss_gdt + state_gdt).astype(jnp.bfloat16)
    partial_value = jnp.dot(grad_x, whole_x.T, preferred_element_type=jnp.float32)
    partial_value = partial_value + jnp.dot(grad_bc, whole_bc.T, preferred_element_type=jnp.float32)
    partial_value = partial_value + jnp.dot(grad_dt, whole_dt.T, preferred_element_type=jnp.float32)
    gradient = lax.psum_scatter(
        partial_value.astype(jnp.bfloat16), TENSOR, scatter_dimension=1, tiled=True
    ).astype(jnp.float32)
    entries = rows * seq_count * gradient.shape[1] * lax.axis_size(TENSOR)
    squares = jnp.sum(gradient * gradient)
    for axis in ("core", "y", "z", "x_lo"):
        squares = lax.psum(squares, axis)
    grad_scale = jnp.sqrt(squares / entries + 1e-06)
    direction = (2 * signs[0] - 1).astype(jnp.float32)[:, None]
    adv = (merged.astype(jnp.float32) + 0.5 * direction * gradient / grad_scale).astype(
        jnp.bfloat16
    )
    picked = adv[local_pos]
    returned = lax.all_to_all(picked, SEQ, split_axis=0, concat_axis=0, tiled=True)
    return (adv[None], returned[None])


def solution(mesh):
    mesh = Mesh(mesh.devices.reshape(2, 2, 8, 4, 2), ("x_hi", "x_lo", "z", "y", "core"))
    return jax.shard_map(
        body,
        mesh=mesh,
        in_specs=(
            P("x_hi", SEQ, TENSOR),
            P("x_hi", SEQ, None),
            P(None, TENSOR),
            P("x_hi", SEQ),
            P("x_hi", SEQ),
            P("x_hi", SEQ),
            P(("x_hi",) + SEQ, TENSOR),
            P(("x_hi",) + SEQ, TENSOR),
            P(("x_hi",) + SEQ, TENSOR),
            P(TENSOR),
            P(TENSOR),
            P(TENSOR),
            P("x_hi", SEQ, TENSOR),
        ),
        out_specs=(P("x_hi", SEQ, TENSOR), P("x_hi", SEQ, TENSOR)),
        check_vma=False,
    )
```

time: 865 us -> 583 us (0.67)
  blocking collectives: 364 us -> 122 us
  other arithmetic: 91.9 us -> 26.2 us
  waiting for transfers between devices: 295 us -> 320 us
    psum x1 -> x4, blocking collectives: 280 us -> 35.6 us  [body(): squares = lax.psum(squares, axis)]
    convert_element_type x33 -> x2, other arithmetic: 40.6 us -> 0.2 us  [the longest x1 0.19 us: carried_in(): part.astype(jnp.bfloat16)]
    select_n x32 -> x9, other arithmetic: 35 us -> 4.33 us  [the longest x8 4.32 us: carried_in(): weights[k] = jnp.where(reached, run, 0.0)]
    all_gather x5, waiting for transfers between devices: 245 us -> 270 us  [the longest x1 135 us: body(): lax.all_gather(w_x, ('x_hi',) + SEQ, axis=0, tiled=True)]
where the time goes in v1:
time: 583 us; the launch traced here: 582 us
  waiting for transfers between devices  320 us (55%)
  blocking collectives  122 us (21%)
  matrix products  62.1 us (11%)
  other arithmetic  26.2 us (4%)
  local copies, waits for them, and re-layouts  18 us (3%)
  between operations  16.6 us (3%)
  starting transfers between devices  16.5 us (3%)
    all_gather x1, waiting for transfers between devices, body(): lax.all_gather(w_x, ('x_hi',) + SEQ, axis=0, tiled=True)  135 us
    all_gather x2, waiting for transfers between devices, carried_in(): lax.all_gather(part.astype(jnp.bfloat16), axis)  77.3 us
    all_gather x1, waiting for transfers between devices, body(): lax.all_gather(w_bc, ('x_hi',) + SEQ, axis=0, tiled=True)  57.8 us
    all_gather x1, blocking collectives, body(): lax.all_gather(w_dt, ('x_hi',) + SEQ, axis=0, tiled=True)  41 us
    psum x4, blocking collectives, body(): squares = lax.psum(squares, axis)  35.6 us
    reduce_scatter x1, waiting for transfers between devices, body(): lax.psum_scatter(partial_value.astype(jnp.bfloat16), TENSOR, scatter_dime...  34.1 us
    all_gather x1, blocking collectives, carried_in(): lax.all_gather(part.astype(jnp.bfloat16), axis)  31.9 us
    dot_general x1, matrix products, body(): proj_x = jnp.dot(features, whole_x, preferred_element_type=jnp.float32)  13.8 us
  transfers between devices with their start and end apart: 9, of which 7 were waited for; matrix products, arithmetic and copies ran while one was open for 8% of the time, Pallas kernels for 0%

profile of v1, /device:TPU:4, one launch (start us, length us, event | category | flops | bytes accessed | tf_op | source)
XLA Modules:
  0.0 581.7 jit_solution(5587890247433560271)
XLA Ops:
  10.9 9.2 %all-to-all-start = ((s32[16,2,1]{1,2,0:T(1,128)}), s32[16,2,1]{1,2,0:T(1,128)S(1)}, u32[]{:S(2)}, u32[]{:S(2)}) async-start(s32[16,2,1]{1,2,0:T(1,128)} %bitcast.1), calls=%async_computation | async-start | bytes 16384 | tf_op jit(solution)/shard_map/all_to_all | solution.py:104
  22.2 6.3 %all-to-all-done = s32[16,2,1]{1,2,0:T(1,128)S(1)} async-done(((s32[16,2,1]{1,2,0:T(1,128)}), s32[16,2,1]{1,2,0:T(1,128)S(1)}, u32[]{:S(2)}, u32[]{:S(2)}) %all-to-all-start) | async-done | bytes 160 | tf_op jit(solution)/shard_map/all_to_all | solution.py:104
  28.5 3.5 all-to-all-start.1
  32.2 8.3 %all-to-all-done.1 = bf16[16,2,1024]{2,1,0:T(2,128)(2,1)S(1)} async-done(((bf16[16,2,1024]{2,1,0:T(2,128)(2,1)}), bf16[16,2,1024]{2,1,0:T(2,128)(2,1)S(1)}, u32[]{:S(2)}, u32[]{:S(2)}) %all-to-all-start.1) | async-done | bytes 65568 | tf_op jit(solution)/shard_map/all_to_all | solution.py:103
  43.6 3.3 collective-permute-start
  47.1 41.0 %all_gather.31 = bf16[8192,16]{0,1:T(8,128)(2,1)S(1)} all-gather(bf16[256,16]{0,1:T(8,128)(2,1)S(1)} %copy-done.20), channel_id=1, replica_groups=mesh['x_hi'=2,'x_lo'=2,'z'=8,'y'=4,'core'=2] {'x_hi','x_lo','z'}, dimensions={0}, use_global_device_ids=true | all-gather | bytes 270336 | tf_op jit(solution)/shard_map/all_gather | solution.py:115
  88.1 1.8 broadcast_compare_fusion
  89.8 2.3 negate_multiply_fusion
  92.5 57.8 %all-gather.11.cloned.1.call-done = bf16[8192,256]{1,0:T(8,128)(2,1)} async-done(((bf16[256,256]{1,0:T(8,128)(2,1)}), bf16[8192,256]{1,0:T(8,128)(2,1)}) %all-gather.11.cloned.1.call-update) | async-done | bytes 4194320 | tf_op jit(solution)/shard_map/all_gather | solution.py:114
  150.3 3.5 fusion.64
  157.8 31.9 %all-gather.2 = bf16[16,1,16]{2,1,0:T(2,128)(2,1)S(1)} all-gather(bf16[1,1,16]{2,1,0:T(2,128)(2,1)S(1)} %bitcast.161), channel_id=1, replica_groups=mesh['x_hi'=2,'x_lo'=2,'z'=8,'y'=4,'core'=2] {'x_lo','z'}, dimensions={0}, use_global_device_ids=true | all-gather | bytes 544 | tf_op jit(solution)/shard_map/all_gather | solution.py:23
  197.0 32.6 %all-gather.15.cloned.1.call-done = bf16[256,64,128]{2,1,0:T(8,128)(2,1)} async-done(((bf16[16,64,128]{2,1,0:T(8,128)(2,1)}), bf16[256,64,128]{2,1,0:T(8,128)(2,1)}) %all-gather.15.cloned.1.call-update) | async-done | bytes 4194320 | tf_op jit(solution)/shard_map/all_gather | solution.py:23
  229.6 3.1 fusion.2
  232.7 135.4 %all-gather.13.cloned.1.call-done = bf16[8192,1024]{1,0:T(8,128)(2,1)} async-done(((bf16[256,1024]{1,0:T(8,128)(2,1)}), bf16[8192,1024]{1,0:T(8,128)(2,1)}) %all-gather.13.cloned.1.call-update) | async-done | bytes 16777232 | tf_op jit(solution)/shard_map/all_gather | solution.py:113
  368.1 13.8 %fusion.66 = f32[128,1024]{0,1:T(8,128)} fusion(bf16[128,8192]{1,0:T(8,128)(2,1)} %all-gather.9.cloned.1.call-done, bf16[8192,1024]{1,0:T(8,128)(2,1)} %all-gather.13.cloned.1.call-done), kind=kOutput, calls=%fused_computation.186 | convolution fusion | flops 2147483648 | bytes 19398656 | tf_op jit(solution)/shard_map/dot_general | solution.py:117
  381.9 4.0 multiply_reduce_fusion.2
  386.5 2.0 fusion.62
  389.1 2.7 convolution_convert_fusion
  400.8 3.2 fusion.14
  408.3 13.7 %fusion.65 = f32[128,8192]{1,0:T(8,128)} fusion(bf16[128,1024]{0,1:T(8,128)(2,1)} %bitcast.157, bf16[8192,1024]{1,0:T(8,128)(2,1)} %all-gather.13.cloned.1.call-done), kind=kOutput, calls=%fused_computation.185 | convolution fusion | flops 2147483648 | bytes 21233664 | tf_op jit(solution)/shard_map/dot_general | solution.py:149
  422.0 44.7 %all-gather.17.cloned.1.call-done = bf16[256,64,128]{2,1,0:T(8,128)(2,1)} async-done(((bf16[16,64,128]{2,1,0:T(8,128)(2,1)}), bf16[256,64,128]{2,1,0:T(8,128)(2,1)}) %all-gather.17.cloned.1.call-update) | async-done | bytes 4194320 | tf_op jit(solution)/shard_map/all_gather | solution.py:23
  466.7 3.1 fusion.1
  470.0 2.1 fusion.7
  479.6 5.1 convolution_add_fusion.1
  484.8 2.2 fusion
  487.0 34.1 %reduce-scatter.2.cloned.1.call-done = bf16[128,1024]{1,0:T(8,128)(2,1)} async-done(((bf16[128,8192]{1,0:T(8,128)(2,1)}), bf16[128,1024]{1,0:T(8,128)(2,1)}) %reduce-scatter.2.cloned.1.call-update) | async-done | bytes 262160 | tf_op jit(solution)/shard_map/reduce_scatter | solution.py:152
  521.0 1.7 fusion.18
  522.7 3.1 psum.28
  525.8 8.8 %psum.29 = f32[]{:T(128)} all-reduce(f32[]{:T(128)} %psum.28), channel_id=1, replica_groups=mesh['x_hi'=2,'x_lo'=2,'z'=8,'y'=4,'core'=2] {'y'}, use_global_device_ids=true, to_apply=%region_16.18 | all-reduce | flops 1 | bytes 8 | tf_op jit(solution)/shard_map/psum | solution.py:158
  534.7 18.1 %psum.30 = f32[]{:T(128)} all-reduce(f32[]{:T(128)} %psum.29), channel_id=1, replica_groups=mesh['x_hi'=2,'x_lo'=2,'z'=8,'y'=4,'core'=2] {'z'}, use_global_device_ids=true, to_apply=%region_17.19 | all-reduce | flops 1 | bytes 8 | tf_op jit(solution)/shard_map/psum | solution.py:158
  552.8 5.6 psum.31
  560.8 13.4 %all_to_all.30 = bf16[16,2,1024]{2,1,0:T(2,128)(2,1)S(1)} all-to-all(bf16[16,2,1024]{2,1,0:T(2,128)(2,1)S(1)} %all_to_all.25), channel_id=1, replica_groups=mesh['x_hi'=2,'x_lo'=2,'z'=8,'y'=4,'core'=2] {'x_lo','z'}, dimensions={0} | all-to-all | bytes 131072 | tf_op jit(solution)/shard_map/all_to_all | solution.py:165
  (162 shorter events, 43.9 us)
Async XLA Ops:
  7.2 12.9 %copy-start = (bf16[1280,1024]{1,0:T(8,128)(2,1)S(1)}, bf16[1280,1024]{1,0:T(8,128)(2,1)}, u32[]{:S(2)}) copy-start(bf16[1280,1024]{1,0:T(8,128)(2,1)} %param.16) | copy-start | bytes 7864324
  7.2 35.8 %copy-start.24 = (s32[1,128]{1,0:T(1,128)S(1)}, s32[1,128]{1,0:T(1,128)}, u32[]{:S(2)}) copy-start(s32[1,128]{1,0:T(1,128)} %param.18) | copy-start | bytes 1540
  7.2 39.9 %copy-start.20 = (bf16[256,16]{0,1:T(8,128)(2,1)S(1)}, bf16[256,16]{0,1:T(8,128)(2,1)}, u32[]{:S(2)}) copy-start(bf16[256,16]{0,1:T(8,128)(2,1)} %param.22) | copy-start | bytes 24580
  7.2 82.6 %copy-start.30 = (f32[16]{0:T(128)S(1)}, f32[16]{0:T(128)}, u32[]{:S(2)}) copy-start(f32[16]{0:T(128)} %param.23) | copy-start | bytes 196
  7.2 82.6 %copy-start.26 = (f32[16]{0:T(128)S(1)}, f32[16]{0:T(128)}, u32[]{:S(2)}) copy-start(f32[16]{0:T(128)} %param.24) | copy-start | bytes 196
  7.2 39.7 %copy-start.8 = (bf16[1,128,1024]{2,1,0:T(8,128)(2,1)S(1)}, bf16[1,128,1024]{2,1,0:T(8,128)(2,1)}, u32[]{:S(2)}) copy-start(bf16[1,128,1024]{2,1,0:T(8,128)(2,1)} %param.26) | copy-start | bytes 786436
  10.9 17.6 %all-to-all-start = ((s32[16,2,1]{1,2,0:T(1,128)}), s32[16,2,1]{1,2,0:T(1,128)S(1)}, u32[]{:S(2)}, u32[]{:S(2)}) async-start(s32[16,2,1]{1,2,0:T(1,128)} %bitcast.1), calls=%async_computation | async-start | bytes 16384 | tf_op jit(solution)/shard_map/all_to_all | solution.py:104
  28.5 12.0 %all-to-all-start.1 = ((bf16[16,2,1024]{2,1,0:T(2,128)(2,1)}), bf16[16,2,1024]{2,1,0:T(2,128)(2,1)S(1)}, u32[]{:S(2)}, u32[]{:S(2)}) async-start(bf16[16,2,1024]{2,1,0:T(2,128)(2,1)} %all_to_all.22), calls=%async_computation.1 | async-start | bytes 131072 | tf_op jit(solution)/shard_map/all_to_all | solution.py:103
  32.0 57.8 %all-gather.9.cloned.1.call-start = ((), (), s32[]{:S(2)}) async-start(), calls=%async_computation.4 | async-start | bytes 2359296 | tf_op jit(solution)/shard_map/all_gather | solution.py:111
  32.2 60.3 %copy-start.28 = (s32[32]{0:T(128)}, s32[32]{0:T(128)S(1)}, u32[]{:S(2)}) copy-start(s32[32]{0:T(128)S(1)} %fusion.58) | copy-start | bytes 388
  42.2 108.1 %all-gather.11.cloned.1.call-start = ((), (), s32[]{:S(2)}) async-start(), calls=%async_computation.5 | async-start | bytes 4325376 | tf_op jit(solution)/shard_map/all_gather | solution.py:114
  42.9 186.6 %all-gather.15.cloned.1.call-start = ((), (), s32[]{:S(2)}) async-start(), calls=%async_computation.8 | async-start | bytes 4456448 | tf_op jit(solution)/shard_map/all_gather | solution.py:23
  43.6 44.5 %collective-permute-start = (s32[1]{0:T(128)}, s32[1]{0:T(128)}, u32[]{:S(2)}, u32[]{:S(2)}) collective-permute-start(s32[1]{0:T(128)} %bitcast.15), channel_id=1, source_target_pairs={{0,8},{8,16},{16,24},{24,32},{32,40},{40,48},{48,56},{56,64},{64,7... | collective-permute-start | bytes 20 | tf_op jit(solution)/shard_map/ppermute | solution.py:18
  88.1 65.7 %copy-start.4 = (bf16[8192,16]{0,1:T(8,128)(2,1)}, bf16[8192,16]{0,1:T(8,128)(2,1)S(1)}, u32[]{:S(2)}) copy-start(bf16[8192,16]{0,1:T(8,128)(2,1)S(1)} %all_gather.31) | copy-start | bytes 786436
  89.8 64.0 %copy-start.25 = (pred[128]{0:T(512)(128)(4,1)}, pred[128]{0:T(512)(128)(4,1)S(1)}, u32[]{:S(2)}) copy-start(pred[128]{0:T(512)(128)(4,1)S(1)} %get-tuple-element.75) | copy-start | bytes 388
  92.5 63.9 %copy-start.15 = (f32[128,16]{0,1:T(8,128)}, f32[128,16]{0,1:T(8,128)S(1)}, u32[]{:S(2)}) copy-start(f32[128,16]{0,1:T(8,128)S(1)} %exponential_select_fusion) | copy-start | bytes 24580
  155.7 212.4 %all-gather.13.cloned.1.call-start = ((), (), s32[]{:S(2)}) async-start(), calls=%async_computation.6 | async-start | bytes 17301504 | tf_op jit(solution)/shard_map/all_gather | solution.py:113
  156.3 310.3 %all-gather.17.cloned.1.call-start = ((), (), s32[]{:S(2)}) async-start(), calls=%async_computation.9 | async-start | bytes 4456448 | tf_op jit(solution)/shard_map/all_gather | solution.py:23
  391.8 129.2 %reduce-scatter.2.cloned.1.call-start = ((), (), s32[]{:S(2)}) async-start(), calls=%async_computation.7 | async-start | bytes 2359296 | tf_op jit(solution)/shard_map/reduce_scatter | solution.py:152
  400.8 5.8 %copy-start.7 = (f32[128,16,64]{0,2,1:T(8,128)S(1)}, f32[128,16,64]{0,2,1:T(8,128)}, u32[]{:S(2)}) copy-start(f32[128,16,64]{0,2,1:T(8,128)} %get-tuple-element.79) | copy-start | bytes 1572868
  400.8 5.8 %copy-start.17 = (f32[128,128]{1,0:T(8,128)S(1)}, f32[128,128]{1,0:T(8,128)}, u32[]{:S(2)}) copy-start(f32[128,128]{1,0:T(8,128)} %copy.122) | copy-start | bytes 196612
  400.8 5.8 %copy-start.18 = (pred[128,128]{1,0:T(8,128)(4,1)S(1)}, pred[128,128]{1,0:T(8,128)(4,1)}, u32[]{:S(2)}) copy-start(pred[128,128]{1,0:T(8,128)(4,1)} %fusion.41) | copy-start | bytes 49156
  400.8 5.8 %copy-start.21 = (f32[128,16]{0,1:T(8,128)S(1)}, f32[128,16]{0,1:T(8,128)}, u32[]{:S(2)}) copy-start(f32[128,16]{0,1:T(8,128)} %get-tuple-element.56) | copy-start | bytes 24580
  400.8 5.8 %copy-start.31 = (f32[16]{0:T(128)S(1)}, f32[16]{0:T(128)}, u32[]{:S(2)}) copy-start(f32[16]{0:T(128)} %param.25) | copy-start | bytes 196
  466.7 5.5 copy-start.16
  466.7 6.5 %copy-start.10 = (f32[128,128]{1,0:T(8,128)S(1)}, f32[128,128]{1,0:T(8,128)}, u32[]{:S(2)}) copy-start(f32[128,128]{1,0:T(8,128)} %copy-done.9) | copy-start | bytes 196612
  479.5 5.1 copy-start.5
  479.6 5.1 copy-start.12
  484.7 49.9 %copy-start.32 = (s32[1,128]{1,0:T(1,128)S(1)}, s32[1,128]{1,0:T(1,128)}, u32[]{:S(2)}) copy-start(s32[1,128]{1,0:T(1,128)} %param.19) | copy-start | bytes 1540
  484.7 68.0 %copy-start.29 = (s32[32]{0:T(128)S(1)}, s32[32]{0:T(128)}, u32[]{:S(2)}) copy-start(s32[32]{0:T(128)} %copy-done.28) | copy-start | bytes 388
  484.8 74.3 %copy-start.3 = (bf16[128,1024]{1,0:T(8,128)(2,1)S(1)}, bf16[128,1024]{1,0:T(8,128)(2,1)}, u32[]{:S(2)}) copy-start(bf16[128,1024]{1,0:T(8,128)(2,1)} %copy-done.2) | copy-start | bytes 786436
  560.1 14.7 %copy-start.6 = (bf16[128,1024]{1,0:T(8,128)(2,1)}, bf16[128,1024]{1,0:T(8,128)(2,1)S(1)}, u32[]{:S(2)}) copy-start(bf16[128,1024]{1,0:T(8,128)(2,1)S(1)} %fusion.17) | copy-start | bytes 786436
  (10 other events, 35.0 us)
Sparse Core Ops, SparseCore 0:
  42.3 24.8 all-gather.8
  69.7 80.4 all-gather.10
  155.9 73.6 all-gather.14
  232.0 136.0 all-gather.12
  391.9 74.6 all-gather.16
  487.1 33.9 reduce-scatter.1

commit v2 on v1

v2 whole, which is shorter than its diff:
```python
import jax
import jax.numpy as jnp
from jax import lax
from jax.experimental import pallas as pl
from jax.experimental.pallas import tpu as pltpu
from jax.sharding import Mesh, PartitionSpec as P

F32, BF16 = jnp.float32, jnp.bfloat16
AXES = ("x_hi", "x_lo", "z", "y", "core")
X = ("x_hi", "x_lo")
SEQ = ("x_lo", "z")
TENSOR = ("y", "core")
CHUNK = 128
WIDE = 1408
HIGH = lax.Precision.HIGHEST
VMEM = pl.BlockSpec(memory_space=pltpu.VMEM)
SMEM = pl.BlockSpec(memory_space=pltpu.SMEM)


def linear(x, z, y, core):
    return ((x * 8 + z) * 4 + y) * 2 + core


def features_route():
    pairs = []
    for x in range(4):
        for z in range(8):
            for y in range(4):
                for core in range(2):
                    there = linear(y, 4 * (z // 4) + x, (z % 4 + x) % 4, core)
                    pairs.append((linear(x, z, y, core), there))
    return pairs


def probe_route():
    pairs = []
    for x in range(4):
        for z in range(8):
            pairs.append((x * 8 + z, (z % 4) * 8 + 4 * (z // 4) + x))
    return pairs


def quarter_route(k):
    pairs = []
    for z in range(8):
        sample, quarter = (z % 4) // 2, 2 * (z % 2) + z // 4
        to = (quarter + k) % 4
        pairs.append((z, 4 * (to % 2) + 2 * sample + to // 2))
    return pairs


def dot_nt(a, b):
    return lax.dot_general(a, b, (((1,), (1,)), ((), ())), preferred_element_type=F32)


def dot_tn(a, b):
    return lax.dot_general(a, b, (((0,), (0,)), ((), ())), preferred_element_type=F32)


def dot_nn(a, b):
    return jnp.dot(a, b, preferred_element_type=F32)


def iota(shape, dim):
    return lax.broadcasted_iota(jnp.int32, shape, dim)


def spread(columns):
    left = iota((CHUNK, 128), 1) < 64
    tiles = [
        jnp.where(left, jnp.broadcast_to(columns[2 * i], (CHUNK, 128)), jnp.broadcast_to(columns[2 * i + 1], (CHUNK, 128)))
        for i in range(2)
    ]
    return jnp.concatenate(tiles, axis=1)


def by_head_rows(values):
    rows = iota((256, 128), 0)
    out = jnp.broadcast_to(values[3], (256, 128))
    for h in (2, 1, 0):
        out = jnp.where(rows < 64 * (h + 1), jnp.broadcast_to(values[h], (256, 128)), out)
    return out


def lanes(row):
    return [row[:, h : h + 1] for h in range(4)]


def weights_of(rows, cols):
    seg = cols[:, 12:13]
    prev, last = rows[13:14, 127:128], rows[12:13, 127:128]
    end = cols[127:128, :]
    carry = jnp.where(seg == prev, jnp.exp(cols), 0.0)
    tail = jnp.where(seg == last, jnp.exp(end - cols), 0.0)
    through = jnp.where(last == prev, jnp.exp(end), 0.0)
    return carry, tail, through


def project_kernel(meta, own, oth, w, out, acc):
    i = pl.program_id(0)
    cols = pl.ds(pl.multiple_of(lax.rem(i, 4) * 256, 256), 256)

    def product(ref):
        rows = jnp.concatenate([ref[lax.rem(k + meta[1], 4), :, cols] for k in range(4)], axis=0)
        return dot_nn(rows, w[0])

    @pl.when(i == 0)
    def _():
        acc[...] = product(own)

    @pl.when((i > 0) & (i < 4))
    def _():
        acc[...] += product(own)

    @pl.when(i >= 4)
    def _():
        acc[...] += product(oth)

    @pl.when(i == 7)
    def _():
        steps = acc[:, 1280:1408].T
        for d in range(4):
            out[d, 0:512, 0:256] = acc[:, 256 * d : 256 * d + 256].astype(BF16)
            out[d, 0:512, 256:512] = acc[:, 1024:1280].astype(BF16)
            mine = jnp.concatenate([steps[4 * d : 4 * d + 4], jnp.zeros((12, 512), F32)], axis=0)
            out[d, 512:528, :] = mine.astype(BF16)


def project(meta, own, oth, w):
    whole = lambda i, m: (0, 0, 0)
    return pl.pallas_call(
        project_kernel,
        out_shape=jax.ShapeDtypeStruct((4, 528, 512), BF16),
        grid_spec=pltpu.PrefetchScalarGridSpec(
            num_scalar_prefetch=1,
            grid=(8,),
            in_specs=[
                pl.BlockSpec((4, 128, 1024), whole),
                pl.BlockSpec((4, 128, 1024), whole),
                pl.BlockSpec((1, 256, WIDE), lambda i, m: (lax.rem(m[0] + i // 4, 2) * 4 + lax.rem(i, 4), 0, 0)),
            ],
            out_specs=pl.BlockSpec((4, 528, 512), whole),
            scratch_shapes=[pltpu.VMEM((512, WIDE), F32)],
        ),
    )(meta, own, oth, w)


def prepare_kernel(meta, r, p, prm, pay, x, bc, rows_out, cols_out, t_out, q_out):
    total = r[0, 0:512, :].astype(F32)
    raw = r[0, 512:528, :].astype(F32)
    for d in range(1, 4):
        total += r[d, 0:512, :].astype(F32)
        raw += r[d, 512:528, :].astype(F32)
    x[...] = total[:, 0:256]
    bc[...] = total[:, 256:512].astype(BF16)
    upper = (iota((128, 128), 0) <= iota((128, 128), 1)).astype(F32)
    top = iota((8, 128), 0) < 4
    bias, rate = prm[0], prm[1]
    through = []
    for k in range(4):
        here = slice(128 * k, 128 * k + 128)
        z = raw[0:8, here] + bias
        dt = jnp.maximum(z, 0.0) + jnp.log1p(jnp.exp(-jnp.abs(z)))
        logs = jnp.dot(-dt * rate, upper, precision=HIGH, preferred_element_type=F32)
        seg = p[k, 128:144, 0:128].astype(F32)[0:8]
        rows = jnp.concatenate([jnp.where(top, logs, pltpu.roll(dt, 4, 0)), jnp.where(top, z, pltpu.roll(seg, 4, 0))], axis=0)
        cols = jnp.concatenate([rows, jnp.zeros((112, 128), F32)], axis=0).T
        rows_out[k] = rows
        cols_out[k] = cols
        carry, tail, thru = weights_of(rows, cols)
        through.append(thru)
        carry_x = spread(lanes(carry))
        tail_x = spread([tail[:, h : h + 1] * cols[:, 4 + h : 5 + h] for h in range(4)])
        b, c = bc[here, 0:128], bc[here, 128:256]
        t_out[k] = dot_tn((x[here, :] * tail_x).astype(BF16), b)
        q_out[k] = dot_tn((p[k, 0:128, :].astype(F32) * carry_x).astype(BF16), c)
    state = t_out[0]
    grad = q_out[3]
    whole = through[0]
    for k in range(1, 4):
        state = by_head_rows(lanes(through[k])) * state + t_out[k]
        grad = by_head_rows(lanes(through[3 - k])) * grad + q_out[3 - k]
        whole = whole * through[k]
    for k in range(1, 4):
        pay[k - 1, 0:256, :] = jnp.where(meta[2] + k < 4, state, grad).astype(BF16)
        pay[k - 1, 256:272, :] = jnp.broadcast_to(whole, (16, 128)).astype(BF16)


def prepare(meta, r, p, prm):
    return pl.pallas_call(
        prepare_kernel,
        in_specs=[SMEM, VMEM, VMEM, VMEM],
        out_specs=[VMEM] * 7,
        out_shape=[
            jax.ShapeDtypeStruct((3, 272, 128), BF16),
            jax.ShapeDtypeStruct((512, 256), F32),
            jax.ShapeDtypeStruct((512, 256), BF16),
            jax.ShapeDtypeStruct((4, 16, 128), F32),
            jax.ShapeDtypeStruct((4, 128, 128), F32),
            jax.ShapeDtypeStruct((4, 256, 128), F32),
            jax.ShapeDtypeStruct((4, 256, 128), F32),
        ],
    )(meta, r, p, prm)


def intra_kernel(x, bc, p, rows_in, cols_in, skip, dx, dbc, e):
    seen = iota((128, 128), 0) >= iota((128, 128), 1)
    lane = iota((128, 128), 1)
    for k in range(4):
        here = slice(128 * k, 128 * k + 128)
        b, c = bc[here, 0:128], bc[here, 128:256]
        rows, cols = rows_in[k], cols_in[k]
        scores = dot_nt(c, b)
        visible = (cols[:, 12:13] == rows[12:13, :]) & seen
        d_scores = jnp.zeros((128, 128), F32)
        by_row = jnp.zeros((128, 128), F32)
        sums = []
        for tile in range(2):
            part = slice(128 * tile, 128 * tile + 128)
            probe = p[k, 0:128, part].astype(F32)
            values = x[here, part].astype(BF16)
            d_values = skip[:, part] * probe
            for a in range(2):
                h = 2 * tile + a
                mine = jnp.where((lane < 64) if a == 0 else (lane >= 64), probe, 0.0).astype(BF16)
                pulled = dot_nt(mine, values)
                decay = jnp.exp(jnp.where(visible, cols[:, h : h + 1] - rows[h : h + 1, :], -1e30))
                steps = rows[4 + h : 5 + h, :]
                weighted = decay * pulled
                decayed = decay * scores
                plain = weighted * scores
                sums.append(jnp.sum(plain, axis=0, keepdims=True))
                by_row = jnp.where(lane == h, jnp.sum(plain * steps, axis=1, keepdims=True), by_row)
                d_scores += weighted * steps
                d_values += dot_tn((decayed * steps).astype(BF16), mine)
            dx[here, part] = d_values
        d_scores = d_scores.astype(BF16)
        dbc[here, 0:128] = dot_tn(d_scores, c)
        dbc[here, 128:256] = dot_nn(d_scores, b)
        sub = iota((8, 128), 0)
        down = jnp.zeros((8, 128), F32)
        for h in range(4):
            down = jnp.where(sub == h, jnp.broadcast_to(sums[h], (8, 128)), down)
        dt = pltpu.roll(rows[0:8], 4, 0)
        e[k, 0:8, :] = down
        e[k, 8:16, :] = by_row.T[0:8] - dt * down


def intra(x, bc, p, rows, cols, skip):
    return pl.pallas_call(
        intra_kernel,
        in_specs=[VMEM] * 6,
        out_specs=[VMEM] * 3,
        out_shape=[
            jax.ShapeDtypeStruct((512, 256), F32),
            jax.ShapeDtypeStruct((512, 256), F32),
            jax.ShapeDtypeStruct((4, 16, 128), F32),
        ],
    )(x, bc, p, rows, cols, skip)


def finish_kernel(meta, r1, r2, r3, x, bc, p, rows_in, cols_in, t_in, q_in, dx, dbc, e, prm, out):
    quarter = meta[2]
    got = (r1, r2, r3)
    parts = [ref[0:256, :].astype(F32) for ref in got]
    decays = [by_head_rows(lanes(ref[256:272, :].astype(F32)[0:1])) for ref in got]

    def total(order):
        out_sum = jnp.zeros((256, 128), F32)
        run = jnp.ones((256, 128), F32)
        for index, valid in order:
            out_sum += jnp.where(valid, run * parts[index], 0.0)
            run = jnp.where(valid, run * decays[index], run)
        return out_sum

    entering = total([(k - 1, quarter - k >= 0) for k in (1, 2, 3)])
    leaving = total([(3 - m, quarter + m <= 3) for m in (1, 2, 3)])
    weights = [weights_of(rows_in[k], cols_in[k]) for k in range(4)]
    through = [by_head_rows(lanes(weights[k][2])) for k in range(4)]
    states, grads = [entering], [leaving]
    for k in range(3):
        states.append(through[k] * states[k] + t_in[k])
        grads.append(through[3 - k] * grads[k] + q_in[3 - k])
    grads = grads[::-1]
    indicator = (iota((8, 256), 1) // 64 == iota((8, 256), 0)).astype(F32)
    lower = (iota((128, 128), 0) >= iota((128, 128), 1)).astype(F32)
    sub, lane = iota((8, 128), 0), iota((8, 128), 1)
    rate = prm[1]

    def by_head(product):
        dims = (((1,), (1,)), ((), ()))
        return lax.dot_general(indicator, product, dims, precision=HIGH, preferred_element_type=F32)

    for k in range(4):
        here = slice(128 * k, 128 * k + 128)
        rows, cols = rows_in[k], cols_in[k]
        carry, tail, thru = weights[k]
        b, c = bc[here, 0:128], bc[here, 128:256]
        carry_x = spread(lanes(carry))
        tail_x = spread(lanes(tail))
        step_x = spread([cols[:, 4 + h : 5 + h] for h in range(4)])
        state, grad = states[k].astype(BF16), grads[k].astype(BF16)
        probe = p[k, 0:128, :].astype(F32) * carry_x
        values = x[here, :] * tail_x
        carried = probe * dot_nt(c, state)
        pulled = dot_nt(b, grad)
        out[here, 0:256] = (dx[here, :] + tail_x * step_x * pulled).astype(BF16)
        d_b = dbc[here, 0:128] + dot_nn((values * step_x).astype(BF16), grad)
        d_c = dbc[here, 128:256] + dot_nn(probe.astype(BF16), state)
        out[here, 256:384] = d_b.astype(BF16)
        out[here, 384:512] = d_c.astype(BF16)
        from_carry = by_head(carried)
        from_tail = by_head(values * pulled)
        dt = pltpu.roll(rows[0:8], 4, 0)
        d_log = e[k, 8:16, :] + from_carry - dt * from_tail
        both = jnp.sum(grads[k] * states[k], axis=1, keepdims=True)
        end = jnp.sum(jnp.where(sub < 4, dt * from_tail, 0.0), axis=1, keepdims=True)
        for h in range(4):
            own = jnp.sum(both[64 * h : 64 * h + 64], axis=0, keepdims=True) * thru[:, h : h + 1]
            end = jnp.where(sub[:, 0:1] == h, end + own, end)
        d_log = jnp.where(lane == 127, d_log + end, d_log)
        d_step = jnp.dot(d_log, lower, precision=HIGH, preferred_element_type=F32)
        d_dt = e[k, 0:8, :] + from_tail - rate * d_step
        z = rows[8:16]
        d_z = jnp.where(sub < 4, d_dt / (1.0 + jnp.exp(-z)), 0.0)
        out[512:528, here] = jnp.concatenate([d_z, jnp.zeros((8, 128), F32)], axis=0).astype(BF16)


def finish(meta, *args):
    return pl.pallas_call(
        finish_kernel,
        in_specs=[SMEM] + [VMEM] * len(args),
        out_specs=VMEM,
        out_shape=jax.ShapeDtypeStruct((528, 512), BF16),
    )(meta, *args)


def pull_kernel(meta, g, w, oth, own, full):
    i = pl.program_id(0)

    @pl.when(i == 0)
    def _():
        shared = g[0, 0:512, 256:512].astype(F32)
        for d in range(4):
            full[:, 256 * d : 256 * d + 256] = g[d, 0:512, 0:256]
            if d:
                shared += g[d, 0:512, 256:512].astype(F32)
        full[:, 1024:1280] = shared.astype(BF16)
        top = iota((8, 512), 0) < 4
        steps = [g[d, 512:528, :].astype(F32)[0:8] for d in range(4)]
        pairs = [jnp.where(top, steps[2 * j], pltpu.roll(steps[2 * j + 1], 4, 0)) for j in range(2)]
        tall = jnp.concatenate(pairs + [jnp.zeros((112, 512), F32)], axis=0)
        full[:, 1280:1408] = tall.T.astype(BF16)

    part = dot_nt(full[...], w[0]).astype(BF16)
    cols = pl.ds(pl.multiple_of(lax.rem(i, 4) * 256, 256), 256)

    def put(ref):
        for k in range(4):
            ref[lax.rem(k + meta[1], 4), :, cols] = part[128 * k : 128 * k + 128]

    @pl.when(i < 4)
    def _():
        put(oth)

    @pl.when(i >= 4)
    def _():
        put(own)


def pull(meta, g, w):
    whole = lambda i, m: (0, 0, 0)
    return pl.pallas_call(
        pull_kernel,
        out_shape=[jax.ShapeDtypeStruct((4, 128, 1024), BF16)] * 2,
        grid_spec=pltpu.PrefetchScalarGridSpec(
            num_scalar_prefetch=1,
            grid=(8,),
            in_specs=[
                pl.BlockSpec((4, 528, 512), whole),
                pl.BlockSpec((1, 256, WIDE), lambda i, m: (lax.rem(m[0] + 1 + i // 4, 2) * 4 + lax.rem(i, 4), 0, 0)),
            ],
            out_specs=[pl.BlockSpec((4, 128, 1024), whole)] * 2,
            scratch_shapes=[pltpu.VMEM((512, WIDE), BF16)],
        ),
    )(meta, g, w)


def to_all(x, axis):
    return lax.all_to_all(jnp.broadcast_to(x[None], (4,) + x.shape), axis, split_axis=0, concat_axis=0)


def shifted(x, axis, k):
    return lax.ppermute(x, axis, [(i, (i + k) % 4) for i in range(4)])


def sum_of_four(x, axis):
    return x + shifted(x, axis, 1) + shifted(x, axis, 2) + shifted(x, axis, 3)


SWAP = [(0, 1), (1, 0)]


def body(tokens, frame_feats, w_proj, frame_pos, segments, signs, w_x, w_bc, w_dt, dt_bias, decay_rate, skip_gain, probe):
    x_at, z_at, core_at = lax.axis_index(X), lax.axis_index("z"), lax.axis_index("core")
    quarter = 2 * lax.rem(z_at, 2) + z_at // 4
    meta = jnp.stack([core_at, lax.rem(z_at, 4), quarter]).astype(jnp.int32)

    w_all = jnp.concatenate([w_x, w_bc, w_dt, jnp.zeros((256, 112), BF16)], axis=1)
    weights = lax.all_gather(w_all, "z")

    frame_emb = jnp.dot(frame_feats[0], w_proj, preferred_element_type=F32).astype(BF16)
    slot = frame_pos[0] - CHUNK * (jnp.arange(32, dtype=jnp.int32) // 2)
    tagged = jnp.concatenate([frame_emb, jnp.broadcast_to(slot.astype(BF16)[:, None], (32, 128))], axis=1)
    arrived = lax.all_to_all(tagged, SEQ, split_axis=0, concat_axis=0, tiled=True)
    local_pos = arrived[:, 1024].astype(jnp.int32)
    merged = tokens[0].at[local_pos].set(arrived[:, :1024])

    moved = lax.ppermute(merged, AXES, features_route())
    own = to_all(moved, "y")
    oth = lax.ppermute(own, "core", SWAP)

    segment = segments[0]
    before = lax.ppermute(segment[-1:], X + ("z",), [(i, i + 1) for i in range(31)])
    ids = jnp.concatenate([segment[None], jnp.broadcast_to(before[None], (15, CHUNK))]).astype(BF16)
    probe_ids = jnp.concatenate([probe[0], jnp.tile(ids, (1, 8))], axis=0)
    probe_ids = lax.ppermute(probe_ids, X + ("z",), probe_route())
    probe_ids = probe_ids.reshape(144, 4, 256).transpose(1, 0, 2)
    probe_ids = lax.all_to_all(probe_ids, X, split_axis=0, concat_axis=0)

    def four(v):
        return lax.dynamic_slice(v, (4 * x_at,), (4,))

    prm = jnp.stack([four(dt_bias), four(decay_rate)])
    prm = jnp.concatenate([prm, jnp.zeros((2, 4), F32)], axis=1)
    prm = jnp.broadcast_to(prm[:, :, None], (2, 8, 128))
    skip = jnp.repeat(four(skip_gain), 64)[None, :]

    partial_proj = project(meta, own, oth, weights)
    received = lax.all_to_all(partial_proj, X, split_axis=0, concat_axis=0)
    pay, values, bc, rows, cols, t_all, q_all = prepare(meta, received, probe_ids, prm)
    got = [lax.ppermute(pay[k - 1], "z", quarter_route(k)) for k in (1, 2, 3)]
    dx, dbc, e = intra(values, bc, probe_ids, rows, cols, skip)
    grads = finish(meta, *got, values, bc, probe_ids, rows, cols, t_all, q_all, dx, dbc, e, prm)
    everyone = to_all(grads, X)
    oth_part, own_part = pull(meta, everyone, weights)
    swapped = lax.ppermute(oth_part, "core", SWAP)
    both = (own_part.astype(F32) + swapped.astype(F32)).astype(BF16)
    pieces = lax.all_to_all(both, "y", split_axis=0, concat_axis=0)
    away = jnp.sum(pieces.astype(F32), axis=0)
    squares = jnp.broadcast_to(jnp.sum(away * away), (8, 128))
    back = [(b, a) for a, b in features_route()]
    gradient = lax.ppermute(away.astype(BF16), AXES, back)
    squares = squares + lax.ppermute(squares, "core", SWAP)
    squares = sum_of_four(squares, X)
    squares = lax.ppermute(squares, AXES, back)[0, 0]

    direction = (2 * signs[0] - 1).astype(F32)[:, None]
    step = 0.5 * direction * gradient.astype(F32)
    picked = (direction.astype(BF16) * gradient)[local_pos]
    high = squares.astype(BF16)
    low = (squares - high.astype(F32)).astype(BF16)
    lane = jnp.arange(128)[None, :]
    tail = jnp.broadcast_to(jnp.where(lane < 64, high, low), (32, 128))
    returned = lax.all_to_all(jnp.concatenate([picked, tail], axis=1), SEQ, split_axis=0, concat_axis=0, tiled=True)
    sums = returned[::2, 1024:].astype(F32)
    entries = 2048 * 8192
    grad_scale = jnp.sqrt((jnp.sum(sums[:, 0]) + jnp.sum(sums[:, 64])) / entries + 1e-06)
    adv = (merged.astype(F32) + step / grad_scale).astype(BF16)
    adv_frames = (frame_emb.astype(F32) + 0.5 * returned[:, :1024].astype(F32) / grad_scale).astype(BF16)
    return (adv[None], adv_frames[None])


def solution(mesh):
    mesh = Mesh(mesh.devices.reshape(2, 2, 8, 4, 2), AXES)
    return jax.shard_map(
        body,
        mesh=mesh,
        in_specs=(
            P("x_hi", SEQ, TENSOR),
            P("x_hi", SEQ, None),
            P(None, TENSOR),
            P("x_hi", SEQ),
            P("x_hi", SEQ),
            P("x_hi", SEQ),
            P(("x_hi",) + SEQ, TENSOR),
            P(("x_hi",) + SEQ, TENSOR),
            P(("x_hi",) + SEQ, TENSOR),
            P(TENSOR),
            P(TENSOR),
            P(TENSOR),
            P("x_hi", SEQ, TENSOR),
        ),
        out_specs=(P("x_hi", SEQ, TENSOR), P("x_hi", SEQ, TENSOR)),
        check_vma=False,
    )
```

time: 583 us -> 309 us (0.53)
  waiting for transfers between devices: 320 us -> 93.9 us
  matrix products: 62.1 us -> 0.55 us
  Pallas kernels: 0 us -> 39.3 us
  blocking collectives: 122 us -> 83.6 us
  starting transfers between devices: 16.5 us -> 53.2 us
  other arithmetic: 26.2 us -> 7.01 us
    all_gather x5 -> x1, waiting for transfers between devices: 270 us -> 0.01 us  [body(): weights = lax.all_gather(w_all, 'z')]
    all_gather x2 -> x0, blocking collectives: 72.9 us -> none  [the longest x1 41 us: body(): lax.all_gather(w_dt, ('x_hi',) + SEQ, axis=0, tiled=True)]
    all_to_all x1 -> x4, blocking collectives: 13.4 us -> 83.6 us  [the longest x2 46.5 us: to_all(): lax.all_to_all(jnp.broadcast_to(x[None], (4,) + x.shape), axis, split_axi...]
    ppermute x1 -> x14, waiting for transfers between devices: 0.01 us -> 61.8 us  [the longest x1 21.6 us: body(): moved = lax.ppermute(merged, AXES, features_route())]
    dot_general x18 -> x1, matrix products: 62.1 us -> 0.55 us  [body(): jnp.dot(frame_feats[0], w_proj, preferred_element_type=F32).astype(BF16)]
    pallas_call x0 -> x5, Pallas kernels: none -> 39.3 us  [the longest x1 11 us: pull(): pl.pallas_call(pull_kernel, out_shape=[jax.ShapeDtypeStruct((4, 128, 1024...]
    psum x4 -> x0, blocking collectives: 35.6 us -> none  [body(): squares = lax.psum(squares, axis)]
    reduce_scatter x1 -> x0, waiting for transfers between devices: 34.1 us -> none  [body(): lax.psum_scatter(partial_value.astype(jnp.bfloat16), TENSOR, scatter_dime...]
  transfers between devices with their start and end apart: 9 -> 18, of which waited for: 7 -> 9; matrix products, arithmetic and copies ran while one was open for 8% -> 2% of each run, Pallas kernels for 0% -> 5%
where the time goes in v2:
time: 309 us; the launch traced here: 308 us
  waiting for transfers between devices  93.9 us (30%)
  blocking collectives  83.6 us (27%)
  starting transfers between devices  53.2 us (17%)
  Pallas kernels  39.3 us (13%)
  between operations  17.8 us (6%)
  local copies, waits for them, and re-layouts  12.4 us (4%)
  other arithmetic  7.01 us (2%)
    all_to_all x2, blocking collectives, to_all(): lax.all_to_all(jnp.broadcast_to(x[None], (4,) + x.shape), axis, split_axi...  46.5 us
    all_to_all x1, waiting for transfers between devices, body(): received = lax.all_to_all(partial_proj, X, split_axis=0, concat_axis=0)  23.6 us
    ppermute x1, waiting for transfers between devices, body(): moved = lax.ppermute(merged, AXES, features_route())  21.6 us
    all_to_all x1, blocking collectives, body(): pieces = lax.all_to_all(both, 'y', split_axis=0, concat_axis=0)  19.4 us
    ppermute x1, waiting for transfers between devices, body(): probe_ids = lax.ppermute(probe_ids, X + ('z',), probe_route())  18.5 us
    all_to_all x1, blocking collectives, body(): lax.all_to_all(tagged, SEQ, split_axis=0, concat_axis=0, tiled=True)  17.7 us
    all_to_all x1, starting transfers between devices, body(): probe_ids = lax.all_to_all(probe_ids, X, split_axis=0, concat_axis=0)  11.7 us
    pallas_call x1, Pallas kernels, pull(): pl.pallas_call(pull_kernel, out_shape=[jax.ShapeDtypeStruct((4, 128, 1024...  11 us
  transfers between devices with their start and end apart: 18, of which 9 were waited for; matrix products, arithmetic and copies ran while one was open for 2% of the time, Pallas kernels for 5%

profile of v2, /device:TPU:4, one launch (start us, length us, event | category | flops | bytes accessed | tf_op | source)
XLA Modules:
  0.0 307.7 jit_solution(7507668378805406169)
XLA Ops:
  8.2 2.0 concatenate.19
  11.0 17.7 %all_to_all.52 = bf16[16,2,1152]{2,1,0:T(2,128)(2,1)S(1)} all-to-all(bf16[16,2,1152]{2,1,0:T(2,128)(2,1)S(1)} %all_to_all.31), channel_id=1, replica_groups=mesh['x_hi'=2,'x_lo'=2,'z'=8,'y'=4,'core'=2] {'x_lo','z'}, dimensions={0} | all-to-all | bytes 147456 | tf_op jit(solution)/shard_map/all_to_all | solution.py:415
  29.7 5.9 %collective-permute-start = (bf16[128,1024]{1,0:T(8,128)(2,1)S(1)}, bf16[128,1024]{1,0:T(8,128)(2,1)S(1)}, u32[]{:S(2)}, u32[]{:S(2)}) collective-permute-start(bf16[128,1024]{1,0:T(8,128)(2,1)S(1)} %scatter_custom_fusion), channel_id=1, source_target_pairs={{0,0},{1,1},{2,64},{3,65},{4,128},{5,129},{6,192},{7,193},{8,2},{9... | collective-permute-start | bytes 786440 | tf_op jit(solution)/shard_map/ppermute | solution.py:419
  35.6 21.6 %collective-permute-done = bf16[128,1024]{1,0:T(8,128)(2,1)S(1)} collective-permute-done((bf16[128,1024]{1,0:T(8,128)(2,1)S(1)}, bf16[128,1024]{1,0:T(8,128)(2,1)S(1)}, u32[]{:S(2)}, u32[]{:S(2)}) %collective-permute-start) | collective-permute-done | bytes 262176 | tf_op jit(solution)/shard_map/ppermute | solution.py:419
  57.3 18.8 %all_to_all.49.own = bf16[4,128,1024]{2,1,0:T(8,128)(2,1)} all-to-all(bf16[4,128,1024]{2,1,0:T(8,128)(2,1)S(1)} %broadcast_in_dim.32), channel_id=1, replica_groups=mesh['x_hi'=2,'x_lo'=2,'z'=8,'y'=4,'core'=2] {'y'}, dimensions={0} | all-to-all | bytes 2097152 | tf_op jit(solution)/shard_map/all_to_all | solution.py:390
  76.7 1.9 collective-permute-start.2
  78.6 5.7 %collective-permute-done.2 = s32[1]{0:T(128)} collective-permute-done((s32[1]{0:T(128)}, s32[1]{0:T(128)}, u32[]{:S(2)}, u32[]{:S(2)}) %collective-permute-start.2) | collective-permute-done | bytes 36 | tf_op jit(solution)/shard_map/ppermute | solution.py:424
  85.1 1.9 collective-permute-start.3
  87.1 18.5 %collective-permute-done.3 = bf16[144,1024]{1,0:T(8,128)(2,1)S(1)} collective-permute-done((bf16[144,1024]{1,0:T(8,128)(2,1)S(1)}, bf16[144,1024]{1,0:T(8,128)(2,1)S(1)}, u32[]{:S(2)}, u32[]{:S(2)}) %collective-permute-start.3) | collective-permute-done | bytes 294944 | tf_op jit(solution)/shard_map/ppermute | solution.py:427
  106.4 11.7 %all-to-all-start.3 = ((bf16[4,144,256]{2,1,0:T(8,128)(2,1)}), bf16[4,144,256]{2,1,0:T(8,128)(2,1)S(1)}, u32[]{:S(2)}, u32[]{:S(2)}) async-start(bf16[4,144,256]{2,1,0:T(8,128)(2,1)} %bitcast.42), calls=%async_computation.3 | async-start | bytes 589824 | tf_op jit(solution)/shard_map/all_to_all | solution.py:429
  118.7 10.6 %shard_map.140 = bf16[4,528,512]{2,1,0:T(8,128)(2,1)} custom-call(s32[3]{0:T(128)} %pad_add_fusion.meta, bf16[4,128,1024]{2,1,0:T(8,128)(2,1)} %all_to_all.49.own, bf16[4,128,1024]{2,1,0:T(8,128)(2,1)} %collective-permute-done.1.oth, bf16[8,256,1408]{2,1,0:T(8,128)(2,1)} %bitcast.44), custom_call_target="tpu_custom_call" | custom-call | tf_op jit(solution)/shard_map/pallas_call | solution.py:131
  129.4 4.8 %all-to-all-start.2 = ((bf16[4,528,512]{2,1,0:T(8,128)(2,1)}), bf16[4,528,512]{2,1,0:T(8,128)(2,1)}, u32[]{:S(2)}, u32[]{:S(2)}) async-start(bf16[4,528,512]{2,1,0:T(8,128)(2,1)} %shard_map.140), calls=%async_computation.2 | async-start | bytes 4325376 | tf_op jit(solution)/shard_map/all_to_all | solution.py:440
  134.3 23.6 %all-to-all-done.2.r = bf16[4,528,512]{2,1,0:T(8,128)(2,1)} async-done(((bf16[4,528,512]{2,1,0:T(8,128)(2,1)}), bf16[4,528,512]{2,1,0:T(8,128)(2,1)}, u32[]{:S(2)}, u32[]{:S(2)}) %all-to-all-start.2) | async-done | bytes 2162720 | tf_op jit(solution)/shard_map/all_to_all | solution.py:440
  158.6 6.1 %shard_map.141 = (bf16[3,272,128]{2,1,0:T(8,128)(2,1)}, f32[512,256]{1,0:T(8,128)}, bf16[512,256]{1,0:T(8,128)(2,1)}, f32[4,16,128]{2,1,0:T(8,128)}, f32[4,128,1...) custom-call(s32[3]{0:T(128)} %pad_add_fusion.meta, bf16[4,528,512]{2,1,0:T(8,128)(2,1)} %all-to-all-done.2.r, ...), custom_call_target="tpu_custom_call" | custom-call | tf_op jit(solution)/shard_map/pallas_call | solution.py:190
  165.6 3.8 %collective-permute-start.4 = (bf16[272,128]{1,0:T(8,128)(2,1)S(1)}, bf16[272,128]{1,0:T(8,128)(2,1)S(1)}, u32[]{:S(2)}, u32[]{:S(2)}) collective-permute-start(bf16[272,128]{1,0:T(8,128)(2,1)S(1)} %get-tuple-element.32), channel_id=1, source_target_pairs={{0,32},{8,40},{16,48},{24,56},{32,8},{40,0},{48,24},{56,16},{1,33}... | collective-permute-start | bytes 208904 | tf_op jit(solution)/shard_map/ppermute | solution.py:442
  169.4 1.3 collective-permute-start.6
  171.5 4.6 %shard_map.142 = (f32[512,256]{1,0:T(8,128)}, f32[512,256]{1,0:T(8,128)}, f32[4,16,128]{2,1,0:T(8,128)}) custom-call(f32[512,256]{1,0:T(8,128)} %get-tuple-element.15.x, bf16[512,256]{1,0:T(8,128)(2,1)} %get-tuple-element.16.bc, bf16[4,144,256]{2,1,0:T(8,128)(2,1)} %copy-done.1, f32[4,16,128]{2,1,0:T(8,128)} %get-tuple-element.17.rows_in, ...), custom_call_target="tpu_custom_call" | custom-call | tf_op jit(solution)/shard_map/pallas_call | solution.py:250
  176.1 2.5 collective-permute-done.6.r3
  179.3 7.0 %shard_map.143 = bf16[528,512]{1,0:T(8,128)(2,1)} custom-call(s32[3]{0:T(128)} %pad_add_fusion.meta, bf16[272,128]{1,0:T(8,128)(2,1)} %copy-done.5, bf16[272,128]{1,0:T(8,128)(2,1)} %copy-done.6, bf16[272,128]{1,0:T(8,128)(2,1)} %copy-done.7, f32[512,256]{1,0:T(8,128)} %get-tuple-element.15.x, bf16[512,256]{1,0:T(8,128)(2,1)} %get-tuple-element.16.bc, ...), custom_call_target="tpu_custom_call" | custom-call | tf_op jit(solution)/shard_map/pallas_call | solution.py:330
  187.5 27.8 %all_to_all.50.g = bf16[4,528,512]{2,1,0:T(8,128)(2,1)} all-to-all(bf16[4,528,512]{2,1,0:T(8,128)(2,1)S(1)} %broadcast_in_dim.69), channel_id=1, replica_groups=mesh['x_hi'=2,'x_lo'=2,'z'=8,'y'=4,'core'=2] {'x_hi','x_lo'}, dimensions={0} | all-to-all | bytes 4325376 | tf_op jit(solution)/shard_map/all_to_all | solution.py:390
  215.2 11.0 %shard_map.144 = (bf16[4,128,1024]{2,1,0:T(8,128)(2,1)}, bf16[4,128,1024]{2,1,0:T(8,128)(2,1)}) custom-call(s32[3]{0:T(128)} %pad_add_fusion.meta, bf16[4,528,512]{2,1,0:T(8,128)(2,1)} %all_to_all.50.g, bf16[8,256,1408]{2,1,0:T(8,128)(2,1)} %bitcast.45), custom_call_target="tpu_custom_call" | custom-call | tf_op jit(solution)/shard_map/pallas_call | solution.py:373
  226.3 2.9 collective-permute-done.7
  229.2 1.6 add_convert_fusion
  230.8 19.4 %all_to_all.51 = bf16[4,128,1024]{2,1,0:T(8,128)(2,1)S(1)} all-to-all(bf16[4,128,1024]{2,1,0:T(8,128)(2,1)S(1)} %add_convert_fusion), channel_id=1, replica_groups=mesh['x_hi'=2,'x_lo'=2,'z'=8,'y'=4,'core'=2] {'y'}, dimensions={0} | all-to-all | bytes 2097152 | tf_op jit(solution)/shard_map/all_to_all | solution.py:449
  253.6 1.7 collective-permute-start.10
  255.3 1.5 collective-permute-start.11
  256.8 2.0 collective-permute-start.12
  258.9 3.2 %collective-permute-start.8 = (bf16[128,1024]{1,0:T(8,128)(2,1)S(1)}, bf16[128,1024]{1,0:T(8,128)(2,1)S(1)}, u32[]{:S(2)}, u32[]{:S(2)}) collective-permute-start(bf16[128,1024]{1,0:T(8,128)(2,1)S(1)} %get-tuple-element.29), channel_id=1, source_target_pairs={{0,0},{1,1},{64,2},{65,3},{128,4},{129,5},{192,6},{193,7},{2,8},{3... | collective-permute-start | bytes 786440 | tf_op jit(solution)/shard_map/ppermute | solution.py:453
  262.7 5.3 %collective-permute-start.13 = (f32[8,128]{1,0:T(8,128)S(1)}, f32[8,128]{1,0:T(8,128)S(1)}, u32[]{:S(2)}, u32[]{:S(2)}) collective-permute-start(f32[8,128]{1,0:T(8,128)S(1)} %add_add_fusion), channel_id=1, source_target_pairs={{0,0},{1,1},{64,2},{65,3},{128,4},{129,5},{192,6},{193,7},{2,8},{3... | collective-permute-start | bytes 12296 | tf_op jit(solution)/shard_map/ppermute | solution.py:456
  268.1 9.3 %collective-permute-done.13 = f32[8,128]{1,0:T(8,128)S(1)} collective-permute-done((f32[8,128]{1,0:T(8,128)S(1)}, f32[8,128]{1,0:T(8,128)S(1)}, u32[]{:S(2)}, u32[]{:S(2)}) %collective-permute-start.13) | collective-permute-done | bytes 4128 | tf_op jit(solution)/shard_map/ppermute | solution.py:456
  280.7 8.1 %all-to-all-start.6 = ((bf16[16,2,1152]{2,1,0:T(2,128)(2,1)}), bf16[16,2,1152]{2,1,0:T(2,128)(2,1)S(1)}, u32[]{:S(2)}, u32[]{:S(2)}) async-start(bf16[16,2,1152]{2,1,0:T(2,128)(2,1)} %all_to_all.39), calls=%async_computation.6 | async-start | bytes 147456 | tf_op jit(solution)/shard_map/all_to_all | solution.py:465
  288.7 8.5 %all-to-all-done.6 = bf16[16,2,1152]{2,1,0:T(2,128)(2,1)S(1)} async-done(((bf16[16,2,1152]{2,1,0:T(2,128)(2,1)}), bf16[16,2,1152]{2,1,0:T(2,128)(2,1)S(1)}, u32[]{:S(2)}, u32[]{:S(2)}) %all-to-all-start.6) | async-done | bytes 73760 | tf_op jit(solution)/shard_map/all_to_all | solution.py:465
  (92 shorter events, 17.7 us)
Async XLA Ops:
  7.2 3.1 %copy-start = (bf16[1280,1024]{1,0:T(8,128)(2,1)S(1)}, bf16[1280,1024]{1,0:T(8,128)(2,1)}, u32[]{:S(2)}) copy-start(bf16[1280,1024]{1,0:T(8,128)(2,1)} %param.15) | copy-start | bytes 7864324
  7.2 3.1 %copy-start.4 = (bf16[1,32,1280]{2,1,0:T(8,128)(2,1)S(1)}, bf16[1,32,1280]{2,1,0:T(8,128)(2,1)}, u32[]{:S(2)}) copy-start(bf16[1,32,1280]{2,1,0:T(8,128)(2,1)} %param.14) | copy-start | bytes 245764
  7.2 3.0 copy-start.10
  7.2 111.5 %all-gather.3.cloned.1.call-start = ((), (), s32[]{:S(2)}) async-start(), calls=%async_computation.7 | async-start | bytes 6488064 | tf_op jit(solution)/shard_map/all_gather | solution.py:410
  10.2 18.6 %copy-start.2 = (bf16[1,128,1024]{2,1,0:T(8,128)(2,1)S(1)}, bf16[1,128,1024]{2,1,0:T(8,128)(2,1)}, u32[]{:S(2)}) copy-start(bf16[1,128,1024]{2,1,0:T(8,128)(2,1)} %param.13) | copy-start | bytes 786436
  10.9 65.2 %copy-start.11 = (s32[1,128]{1,0:T(1,128)S(1)}, s32[1,128]{1,0:T(1,128)}, u32[]{:S(2)}) copy-start(s32[1,128]{1,0:T(1,128)} %param.17) | copy-start | bytes 1540
  10.9 74.2 %copy-start.3 = (bf16[1,128,1024]{2,1,0:T(8,128)(2,1)S(1)}, bf16[1,128,1024]{2,1,0:T(8,128)(2,1)}, u32[]{:S(2)}) copy-start(bf16[1,128,1024]{2,1,0:T(8,128)(2,1)} %param.25) | copy-start | bytes 786436
  29.7 27.5 %collective-permute-start = (bf16[128,1024]{1,0:T(8,128)(2,1)S(1)}, bf16[128,1024]{1,0:T(8,128)(2,1)S(1)}, u32[]{:S(2)}, u32[]{:S(2)}) collective-permute-start(bf16[128,1024]{1,0:T(8,128)(2,1)S(1)} %scatter_custom_fusion), channel_id=1, source_target_pairs={{0,0},{1,1},{2,64},{3,65},{4,128},{5,129},{6,192},{7,193},{8,2},{9... | collective-permute-start | bytes 786440 | tf_op jit(solution)/shard_map/ppermute | solution.py:419
  76.1 42.6 %collective-permute-start.1 = (bf16[4,128,1024]{2,1,0:T(8,128)(2,1)}, bf16[4,128,1024]{2,1,0:T(8,128)(2,1)}, u32[]{:S(2)}, u32[]{:S(2)}) collective-permute-start(bf16[4,128,1024]{2,1,0:T(8,128)(2,1)} %all_to_all.49.own), channel_id=1, source_target_pairs={{0,1},{1,0},{2,3},{3,2},{4,5},{5,4},{6,7},{7,6},{8,9},{9,8},{10,11... | collective-permute-start | bytes 3145736 | tf_op jit(solution)/shard_map/ppermute | solution.py:421
  76.7 7.6 %collective-permute-start.2 = (s32[1]{0:T(128)}, s32[1]{0:T(128)}, u32[]{:S(2)}, u32[]{:S(2)}) collective-permute-start(s32[1]{0:T(128)} %bitcast.9), channel_id=1, source_target_pairs={{0,8},{8,16},{16,24},{24,32},{32,40},{40,48},{48,56},{56,64},{64,7... | collective-permute-start | bytes 20 | tf_op jit(solution)/shard_map/ppermute | solution.py:424
  85.1 20.5 %collective-permute-start.3 = (bf16[144,1024]{1,0:T(8,128)(2,1)S(1)}, bf16[144,1024]{1,0:T(8,128)(2,1)S(1)}, u32[]{:S(2)}, u32[]{:S(2)}) collective-permute-start(bf16[144,1024]{1,0:T(8,128)(2,1)S(1)} %pad_maximum_fusion), channel_id=1, source_target_pairs={{0,0},{8,64},{16,128},{24,192},{32,32},{40,96},{48,160},{56,224},{... | collective-permute-start | bytes 884744 | tf_op jit(solution)/shard_map/ppermute | solution.py:427
  106.4 23.0 %all-to-all-start.3 = ((bf16[4,144,256]{2,1,0:T(8,128)(2,1)}), bf16[4,144,256]{2,1,0:T(8,128)(2,1)S(1)}, u32[]{:S(2)}, u32[]{:S(2)}) async-start(bf16[4,144,256]{2,1,0:T(8,128)(2,1)} %bitcast.42), calls=%async_computation.3 | async-start | bytes 589824 | tf_op jit(solution)/shard_map/all_to_all | solution.py:429
  129.3 4.8 %copy-start.8 = (f32[16]{0:T(128)S(1)}, f32[16]{0:T(128)}, u32[]{:S(2)}) copy-start(f32[16]{0:T(128)} %param.23) | copy-start | bytes 196
  129.3 4.8 %copy-start.9 = (f32[16]{0:T(128)S(1)}, f32[16]{0:T(128)}, u32[]{:S(2)}) copy-start(f32[16]{0:T(128)} %param.22) | copy-start | bytes 196
  129.3 4.8 %copy-start.1 = (bf16[4,144,256]{2,1,0:T(8,128)(2,1)}, bf16[4,144,256]{2,1,0:T(8,128)(2,1)S(1)}, u32[]{:S(2)}) copy-start(bf16[4,144,256]{2,1,0:T(8,128)(2,1)S(1)} %all-to-all-done.3.p) | copy-start | bytes 884740
  129.4 28.5 %all-to-all-start.2 = ((bf16[4,528,512]{2,1,0:T(8,128)(2,1)}), bf16[4,528,512]{2,1,0:T(8,128)(2,1)}, u32[]{:S(2)}, u32[]{:S(2)}) async-start(bf16[4,528,512]{2,1,0:T(8,128)(2,1)} %shard_map.140), calls=%async_computation.2 | async-start | bytes 4325376 | tf_op jit(solution)/shard_map/all_to_all | solution.py:440
  134.2 36.6 %copy-start.12 = (f32[16]{0:T(128)S(1)}, f32[16]{0:T(128)}, u32[]{:S(2)}) copy-start(f32[16]{0:T(128)} %param.24) | copy-start | bytes 196
  165.6 10.5 %collective-permute-start.4 = (bf16[272,128]{1,0:T(8,128)(2,1)S(1)}, bf16[272,128]{1,0:T(8,128)(2,1)S(1)}, u32[]{:S(2)}, u32[]{:S(2)}) collective-permute-start(bf16[272,128]{1,0:T(8,128)(2,1)S(1)} %get-tuple-element.32), channel_id=1, source_target_pairs={{0,32},{8,40},{16,48},{24,56},{32,8},{40,0},{48,24},{56,16},{1,33}... | collective-permute-start | bytes 208904 | tf_op jit(solution)/shard_map/ppermute | solution.py:442
  169.4 6.7 %collective-permute-start.5 = (bf16[272,128]{1,0:T(8,128)(2,1)S(1)}, bf16[272,128]{1,0:T(8,128)(2,1)S(1)}, u32[]{:S(2)}, u32[]{:S(2)}) collective-permute-start(bf16[272,128]{1,0:T(8,128)(2,1)S(1)} %get-tuple-element.31), channel_id=1, source_target_pairs={{0,8},{8,0},{16,24},{24,16},{32,40},{40,32},{48,56},{56,48},{1,9},... | collective-permute-start | bytes 208904 | tf_op jit(solution)/shard_map/ppermute | solution.py:442
  169.4 9.2 %collective-permute-start.6 = (bf16[272,128]{1,0:T(8,128)(2,1)S(1)}, bf16[272,128]{1,0:T(8,128)(2,1)S(1)}, u32[]{:S(2)}, u32[]{:S(2)}) collective-permute-start(bf16[272,128]{1,0:T(8,128)(2,1)S(1)} %get-tuple-element.30), channel_id=1, source_target_pairs={{0,40},{8,32},{16,56},{24,48},{32,0},{40,8},{48,16},{56,24},{1,41}... | collective-permute-start | bytes 208904 | tf_op jit(solution)/shard_map/ppermute | solution.py:442
  176.1 2.5 copy-start.5
  176.1 2.5 copy-start.6
  178.6 0.6 copy-start.7
  226.3 2.9 collective-permute-start.7
  230.8 28.1 %copy-start.13 = (s32[1,128]{1,0:T(1,128)S(1)}, s32[1,128]{1,0:T(1,128)}, u32[]{:S(2)}) copy-start(s32[1,128]{1,0:T(1,128)} %param.18) | copy-start | bytes 1540
  251.7 1.3 collective-permute-start.9
  253.6 8.4 %collective-permute-start.10 = (f32[8,128]{1,0:T(8,128)S(1)}, f32[8,128]{1,0:T(8,128)S(1)}, u32[]{:S(2)}, u32[]{:S(2)}) collective-permute-start(f32[8,128]{1,0:T(8,128)S(1)} %broadcast_add_fusion), channel_id=1, source_target_pairs={{0,64},{64,128},{128,192},{192,0},{1,65},{65,129},{129,193},{193,1... | collective-permute-start | bytes 12296 | tf_op jit(solution)/shard_map/ppermute | solution.py:394
  255.3 6.7 %collective-permute-start.11 = (f32[8,128]{1,0:T(8,128)S(1)}, f32[8,128]{1,0:T(8,128)S(1)}, u32[]{:S(2)}, u32[]{:S(2)}) collective-permute-start(f32[8,128]{1,0:T(8,128)S(1)} %broadcast_add_fusion), channel_id=1, source_target_pairs={{0,128},{64,192},{128,0},{192,64},{1,129},{65,193},{129,1},{193,65... | collective-permute-start | bytes 12296 | tf_op jit(solution)/shard_map/ppermute | solution.py:394
  256.8 5.3 %collective-permute-start.12 = (f32[8,128]{1,0:T(8,128)S(1)}, f32[8,128]{1,0:T(8,128)S(1)}, u32[]{:S(2)}, u32[]{:S(2)}) collective-permute-start(f32[8,128]{1,0:T(8,128)S(1)} %broadcast_add_fusion), channel_id=1, source_target_pairs={{0,192},{64,0},{128,64},{192,128},{1,193},{65,1},{129,65},{193,129... | collective-permute-start | bytes 12296 | tf_op jit(solution)/shard_map/ppermute | solution.py:394
  258.9 20.4 %collective-permute-start.8 = (bf16[128,1024]{1,0:T(8,128)(2,1)S(1)}, bf16[128,1024]{1,0:T(8,128)(2,1)S(1)}, u32[]{:S(2)}, u32[]{:S(2)}) collective-permute-start(bf16[128,1024]{1,0:T(8,128)(2,1)S(1)} %get-tuple-element.29), channel_id=1, source_target_pairs={{0,0},{1,1},{64,2},{65,3},{128,4},{129,5},{192,6},{193,7},{2,8},{3... | collective-permute-start | bytes 786440 | tf_op jit(solution)/shard_map/ppermute | solution.py:453
  262.7 14.6 %collective-permute-start.13 = (f32[8,128]{1,0:T(8,128)S(1)}, f32[8,128]{1,0:T(8,128)S(1)}, u32[]{:S(2)}, u32[]{:S(2)}) collective-permute-start(f32[8,128]{1,0:T(8,128)S(1)} %add_add_fusion), channel_id=1, source_target_pairs={{0,0},{1,1},{64,2},{65,3},{128,4},{129,5},{192,6},{193,7},{2,8},{3... | collective-permute-start | bytes 12296 | tf_op jit(solution)/shard_map/ppermute | solution.py:456
  280.7 16.6 %all-to-all-start.6 = ((bf16[16,2,1152]{2,1,0:T(2,128)(2,1)}), bf16[16,2,1152]{2,1,0:T(2,128)(2,1)S(1)}, u32[]{:S(2)}, u32[]{:S(2)}) async-start(bf16[16,2,1152]{2,1,0:T(2,128)(2,1)} %all_to_all.39), calls=%async_computation.6 | async-start | bytes 147456 | tf_op jit(solution)/shard_map/all_to_all | solution.py:465
Sparse Core Ops, SparseCore 0:
  10.3 79.8 all-gather.2
